TPU v7x, 512 devices: a whole 4x4x16 slice. The times are simulated.
512 devices in a mesh: phi: 64 (over y, x, z_hi, core), row: 8 (over z_lo).
Axes of the slice: x: 4, y: 4, z: 16 (z_hi: 2, z_lo: 8; z = z_hi * 8 + z_lo), core: 2. Of those that a mesh axis runs over, the one named last changes fastest.
Arguments:
- magnetogram: bfloat16 [16384, 1024], P('phi', 'row'), may hold values from -6 to 6
- col_owner: int32 [16384], P('phi'), may hold values from 0 to 63, as said below
- col_offset: int32 [16384], P('phi'), may hold values from 0 to 7, as said below
- phi_weight: bfloat16 [512, 3072], P(None, 'phi'), may hold values from -0.375 to 0.375
- theta_weight: bfloat16 [1024, 128], P('row'), may hold values from -0.1875 to 0.1875
- radial_coef: float32 [32], replicated, may hold values from 0.3 to 3
- theta_coef: float32 [128], replicated, may hold values from 0.3 to 3
- phi_coef: float32 [3072], replicated, may hold values from 0.3 to 3
- start_field: float32 [32, 3072, 128], P('row', 'phi'), may hold values from -0.3125 to 0.3125
Outputs:
- solution_field: float32 [32, 3072, 128], P('row', 'phi')
- residual: float32 [32, 3072, 128], P('row', 'phi')
Inputs may be any that keep to these rules, and one draw needn't show every extreme that they name: `col_owner`: within each aligned block of 256 columns (the columns of one index of phi) at most 8 columns share an owner, and one owner receives exactly 8 columns from every block. `col_offset`: columns of one aligned block of 256 columns that share an owner have distinct offsets.
All inputs are finite; a program needn't handle non-finite values.
Results may differ from a plain program's by a relative error of at most 0.019.
Values may be sent and summed in bfloat16 or wider, within the bound.
A program may use at most 64 MiB of HBM per device.

v0:
```python
import jax
import jax.numpy as jnp
from jax import lax
from jax.sharding import PartitionSpec as P

ITERS = 2


def with_halo(block, sides, width, periodic):
    for axis, dim in sides:
        count = lax.axis_size(axis)
        forward = [(i, i + 1) for i in range(count - 1)]
        if periodic:
            forward.append((count - 1, 0))
        backward = [(target, source) for source, target in forward]
        low = lax.ppermute(
            lax.slice_in_dim(block, block.shape[dim] - width, None, axis=dim), axis, forward
        )
        high = lax.ppermute(lax.slice_in_dim(block, 0, width, axis=dim), axis, backward)
        block = jnp.concatenate([low, block, high], axis=dim)
    return block


def face_coefs(radial_coef, theta_coef, phi_coef):
    radial_mid = 0.5 * (radial_coef[:-1] + radial_coef[1:])
    radial_upper = jnp.concatenate([radial_mid, radial_coef[-1:]])
    radial_lower = jnp.concatenate([radial_coef[:1], radial_mid])
    theta_mid = 0.5 * (theta_coef[:-1] + theta_coef[1:])
    zero_one = jnp.zeros((1,), jnp.float32)
    theta_upper = jnp.concatenate([theta_mid, zero_one])
    theta_lower = jnp.concatenate([zero_one, theta_mid])
    phi_upper = 0.5 * (phi_coef + jnp.roll(phi_coef, -1))
    phi_lower = jnp.roll(phi_upper, 1)
    return (radial_upper, radial_lower, theta_upper, theta_lower, phi_upper, phi_lower)


def split_product(form, data, weight):
    upper_part = data.astype(jnp.bfloat16)
    remainder = data - lax.optimization_barrier(upper_part).astype(jnp.float32)
    middle_part = remainder.astype(jnp.bfloat16)
    remainder = remainder - lax.optimization_barrier(middle_part).astype(jnp.float32)
    lower_part = remainder.astype(jnp.bfloat16)
    total = jnp.einsum(form, upper_part, weight, preferred_element_type=jnp.float32)
    total = total + jnp.einsum(form, middle_part, weight, preferred_element_type=jnp.float32)
    return total + jnp.einsum(form, lower_part, weight, preferred_element_type=jnp.float32)


def precond_total(residual, precond):
    return lax.psum(jnp.sum(residual * precond), ("phi", "row"))


def body(
    magnetogram,
    col_owner,
    col_offset,
    phi_weight,
    theta_weight,
    radial_coef,
    theta_coef,
    phi_coef,
    start_field,
):
    layers, cells, width = start_field.shape
    phi_devices = lax.axis_size("phi")
    slots = phi_weight.shape[0]
    capacity = slots // phi_devices
    faces = face_coefs(radial_coef, theta_coef, phi_coef)
    row_start = lax.axis_index("row") * layers
    phi_start = lax.axis_index("phi") * cells
    rad_upper = lax.dynamic_slice_in_dim(faces[0], row_start, layers)[:, None, None]
    rad_lower = lax.dynamic_slice_in_dim(faces[1], row_start, layers)[:, None, None]
    lat_upper = faces[2][None, None, :]
    lat_lower = faces[3][None, None, :]
    lon_upper = lax.dynamic_slice_in_dim(faces[4], phi_start, cells)[None, :, None]
    lon_lower = lax.dynamic_slice_in_dim(faces[5], phi_start, cells)[None, :, None]
    inv_diag = 1.0 / (rad_upper + rad_lower + lat_upper + lat_lower + lon_upper + lon_lower)

    def apply_operator(field):
        phi_pad = with_halo(field, (("phi", 1),), 1, True)
        radial_pad = with_halo(field, (("row", 0),), 1, False)
        theta_pad = jnp.pad(field, ((0, 0), (0, 0), (1, 1)))
        result = rad_upper * (field - radial_pad[2:]) + rad_lower * (field - radial_pad[:-2])
        result = (
            result
            + lat_upper * (field - theta_pad[:, :, 2:])
            + lat_lower * (field - theta_pad[:, :, :-2])
        )
        result = (
            result + lon_upper * (field - phi_pad[:, 2:]) + lon_lower * (field - phi_pad[:, :-2])
        )
        return result

    destination = col_owner * capacity + col_offset
    matching = destination[None, :] == jnp.arange(slots, dtype=jnp.int32)[:, None]
    column_ids = jnp.arange(destination.shape[0], dtype=jnp.int32)
    slot_column = jnp.sum(jnp.where(matching, column_ids[None, :], 0), axis=1)
    filled = jnp.any(matching, axis=1)[:, None]
    blocks = phi_weight.reshape(phi_devices, capacity, cells)
    packed = jnp.where(
        filled, jnp.take(magnetogram, slot_column, axis=0), jnp.zeros((), jnp.bfloat16)
    )
    packed = packed.reshape(phi_devices, capacity, -1)
    partial_lon = jnp.einsum(
        "sck,scm->km",
        blocks,
        lax.all_to_all(packed, "phi", split_axis=0, concat_axis=0, tiled=True),
        preferred_element_type=jnp.float32,
    )
    partial_bnd = split_product("km,mj->kj", partial_lon, theta_weight)
    boundary = lax.psum(partial_bnd, "row")
    inner_flag = (lax.axis_index("row") == 0).astype(jnp.float32)
    inner_layer = (inner_flag * rad_lower[0] * boundary)[None]
    right_side = jnp.concatenate(
        [inner_layer, jnp.zeros((layers - 1, cells, width), jnp.float32)], axis=0
    )
    solution_field = start_field
    residual = right_side - apply_operator(start_field)
    precond = residual * inv_diag
    direction = precond
    norm_now = precond_total(residual, precond)
    for sweep_index in range(ITERS):
        image = apply_operator(direction)
        alpha = norm_now / lax.psum(jnp.sum(direction * image), ("phi", "row"))
        solution_field = solution_field + alpha * direction
        residual = residual - alpha * image
        if sweep_index + 1 < ITERS:
            precond = residual * inv_diag
            norm_next = precond_total(residual, precond)
            direction = precond + norm_next / norm_now * direction
            norm_now = norm_next
    return (solution_field, residual)


def solution(mesh):
    in_specs = (
        P("phi", "row"),
        P("phi"),
        P("phi"),
        P(None, "phi"),
        P("row", None),
        P(),
        P(),
        P(),
        P("row", "phi", None),
    )
    out_specs = (P("row", "phi", None), P("row", "phi", None))
    return jax.shard_map(body, mesh=mesh, in_specs=in_specs, out_specs=out_specs, check_vma=False)
```

profile of v0, /device:TPU:1, one launch (start us, length us, event | category | flops | bytes accessed | tf_op | source)
XLA Modules:
  0.0 478.4 jit_solution(5889588120219888219)
XLA Ops:
  0.6 0.0 copy-start
  0.6 0.8 fusion.69
  1.4 8.8 %collective-permute-start.2 = (f32[4,1,128]{2,1,0:T(1,128)S(1)}, f32[4,1,128]{2,1,0:T(1,128)S(1)}, u32[]{:S(2)}, u32[]{:S(2)}) collective-permute-start(f32[4,1,128]{2,1,0:T(1,128)S(1)} %get-tuple-element.26), channel_id=1, source_target_pairs={{8,0},{16,8},{24,16},{32,24},{40,32},{48,40},{56,48},{64,56},{72,6... | collective-permute-start | bytes 6152 | tf_op jit(solution)/shard_map/ppermute | solution.py:19
  10.2 10.0 %collective-permute-start.3 = (f32[4,1,128]{2,1,0:T(1,128)S(1)}, f32[4,1,128]{2,1,0:T(1,128)S(1)}, u32[]{:S(2)}, u32[]{:S(2)}) collective-permute-start(f32[4,1,128]{2,1,0:T(1,128)S(1)} %get-tuple-element.27), channel_id=1, source_target_pairs={{0,8},{8,16},{16,24},{24,32},{32,40},{40,48},{48,56},{56,64},{64,7... | collective-permute-start | bytes 6152 | tf_op jit(solution)/shard_map/ppermute | solution.py:16
  20.2 0.8 fusion.68
  20.9 1.4 collective-permute-start
  22.4 4.0 collective-permute-start.1
  26.4 0.2 fusion
  26.6 0.2 select_reduce_fusion
  26.7 0.1 reduce_sum.50
  26.8 0.1 broadcast_in_dim.50
  27.0 1.3 gather_fusion
  28.3 0.9 fusion.2
  29.2 21.1 %all-to-all-start = ((bf16[64,8,128]{2,1,0:T(8,128)(2,1)}), bf16[64,8,128]{2,1,0:T(8,128)(2,1)S(1)}, u32[]{:S(2)}, u32[]{:S(2)}) async-start(bf16[64,8,128]{2,1,0:T(8,128)(2,1)} %fusion.2), calls=%async_computation | async-start | bytes 262144 | tf_op jit(solution)/shard_map/all_to_all | solution.py:106
  50.3 0.0 copy-start.4
  50.3 0.1 add_multiply_fusion.1
  50.4 0.6 fusion.70
  51.0 0.6 slice.154
  51.6 0.1 slice.153
  51.6 0.8 fusion.58
  52.4 0.7 slice.183
  53.1 0.1 dynamic_slice.14
  53.1 0.1 copy.20
  53.3 0.8 fusion.59
  54.0 1.4 pad_maximum_fusion.12
  55.4 0.1 fusion.63
  55.5 0.6 copy-done.8
  56.1 0.1 add_multiply_fusion
  56.2 0.1 pad_maximum_fusion.14
  56.3 0.1 add_add_fusion
  56.4 11.2 %all-to-all-done = bf16[64,8,128]{2,1,0:T(8,128)(2,1)S(1)} async-done(((bf16[64,8,128]{2,1,0:T(8,128)(2,1)}), bf16[64,8,128]{2,1,0:T(8,128)(2,1)S(1)}, u32[]{:S(2)}, u32[]{:S(2)}) %all-to-all-start) | async-done | bytes 131104 | tf_op jit(solution)/shard_map/all_to_all | solution.py:106
  67.6 0.2 fusion.71
  67.8 0.0 copy-start.2
  67.8 0.7 copy-done.2
  68.6 0.1 fusion.72
  68.7 0.1 convolution_add_fusion.1
  68.8 0.1 convolution_add_fusion
  69.0 46.3 %psum.35 = f32[48,128]{1,0:T(8,128)S(1)} all-reduce(f32[48,128]{1,0:T(8,128)S(1)} %convolution_add_fusion), channel_id=1, replica_groups=mesh['phi'=64,'row'=8] {'row'}, use_global_device_ids=true, to_apply=%region_2.3 | all-reduce | flops 6144 | bytes 49152 | tf_op jit(solution)/shard_map/psum | solution.py:110
  115.3 0.0 collective-permute-done.2
  115.3 0.0 collective-permute-done.3
  115.3 0.0 collective-permute-done
  115.4 0.0 collective-permute-done.1
  115.4 0.2 fusion.56
  115.6 1.3 collective-permute-start.4
  116.9 4.0 collective-permute-start.5
  120.9 7.9 %collective-permute-start.6 = (f32[4,1,128]{2,1,0:T(1,128)S(1)}, f32[4,1,128]{2,1,0:T(1,128)S(1)}, u32[]{:S(2)}, u32[]{:S(2)}) collective-permute-start(f32[4,1,128]{2,1,0:T(1,128)S(1)} %get-tuple-element.22), channel_id=1, source_target_pairs={{8,0},{16,8},{24,16},{32,24},{40,32},{48,40},{56,48},{64,56},{72,6... | collective-permute-start | bytes 6152 | tf_op jit(solution)/shard_map/ppermute | solution.py:19
  128.8 6.3 %collective-permute-start.7 = (f32[4,1,128]{2,1,0:T(1,128)S(1)}, f32[4,1,128]{2,1,0:T(1,128)S(1)}, u32[]{:S(2)}, u32[]{:S(2)}) collective-permute-start(f32[4,1,128]{2,1,0:T(1,128)S(1)} %get-tuple-element.23), channel_id=1, source_target_pairs={{0,8},{8,16},{16,24},{24,32},{32,40},{40,48},{48,56},{56,64},{64,7... | collective-permute-start | bytes 6152 | tf_op jit(solution)/shard_map/ppermute | solution.py:16
  135.2 0.7 collective-permute-done.7
  135.9 0.8 multiply_reduce_fusion.2
  136.6 107.3 %all-reduce.4 = (f32[]{:T(128)}, f32[]{:T(128)}) all-reduce(f32[]{:T(128)} %get-tuple-element.3, f32[]{:T(128)} %get-tuple-element.2), channel_id=1, replica_groups=mesh['phi'=64,'row'=8] {'phi','row'}, use_global_device_ids=true, to_apply=%region_4.5 | all-reduce | flops 2 | bytes 16 | tf_op jit(solution)/shard_map/psum | solution.py:49
  245.3 0.7 multiply_reduce_fusion.1
  246.0 100.5 %psum.38 = f32[]{:T(128)} all-reduce(f32[]{:T(128)} %get-tuple-element.8), channel_id=1, replica_groups=mesh['phi'=64,'row'=8] {'phi','row'}, use_global_device_ids=true, to_apply=%region_8.9 | all-reduce | flops 1 | bytes 8 | tf_op jit(solution)/shard_map/psum | solution.py:49
  347.8 0.1 multiply_add_fusion.1
  347.9 1.3 collective-permute-start.8
  349.2 4.0 collective-permute-start.9
  353.2 3.1 collective-permute-start.10
  356.3 11.2 %collective-permute-start.11 = (f32[4,1,128]{2,1,0:T(1,128)S(1)}, f32[4,1,128]{2,1,0:T(1,128)S(1)}, u32[]{:S(2)}, u32[]{:S(2)}) collective-permute-start(f32[4,1,128]{2,1,0:T(1,128)S(1)} %get-tuple-element.19), channel_id=1, source_target_pairs={{0,8},{8,16},{16,24},{24,32},{32,40},{40,48},{48,56},{56,64},{64,7... | collective-permute-start | bytes 6152 | tf_op jit(solution)/shard_map/ppermute | solution.py:16
  367.5 0.0 collective-permute-done.10
  367.5 0.7 collective-permute-done.11
  368.2 0.0 collective-permute-done.8
  368.2 0.0 collective-permute-done.9
  368.2 0.7 multiply_reduce_fusion
  369.0 107.4 %psum.39 = f32[]{:T(128)} all-reduce(f32[]{:T(128)} %get-tuple-element.6), channel_id=1, replica_groups=mesh['phi'=64,'row'=8] {'phi','row'}, use_global_device_ids=true, to_apply=%region_10.11 | all-reduce | flops 1 | bytes 8 | tf_op jit(solution)/shard_map/psum | solution.py:123
  477.7 0.7 multiply_subtract_fusion
  (26 shorter events, 0.1 us)
Async XLA Ops:
  0.6 26.3 %copy-start = (bf16[256,128]{1,0:T(8,128)(2,1)S(1)}, bf16[256,128]{1,0:T(8,128)(2,1)}, u32[]{:S(2)}) copy-start(bf16[256,128]{1,0:T(8,128)(2,1)} %param.9) | copy-start | bytes 196612
  1.4 113.9 %collective-permute-start.2 = (f32[4,1,128]{2,1,0:T(1,128)S(1)}, f32[4,1,128]{2,1,0:T(1,128)S(1)}, u32[]{:S(2)}, u32[]{:S(2)}) collective-permute-start(f32[4,1,128]{2,1,0:T(1,128)S(1)} %get-tuple-element.26), channel_id=1, source_target_pairs={{8,0},{16,8},{24,16},{32,24},{40,32},{48,40},{56,48},{64,56},{72,6... | collective-permute-start | bytes 6152 | tf_op jit(solution)/shard_map/ppermute | solution.py:19
  10.2 105.1 %collective-permute-start.3 = (f32[4,1,128]{2,1,0:T(1,128)S(1)}, f32[4,1,128]{2,1,0:T(1,128)S(1)}, u32[]{:S(2)}, u32[]{:S(2)}) collective-permute-start(f32[4,1,128]{2,1,0:T(1,128)S(1)} %get-tuple-element.27), channel_id=1, source_target_pairs={{0,8},{8,16},{16,24},{24,32},{32,40},{40,48},{48,56},{56,64},{64,7... | collective-permute-start | bytes 6152 | tf_op jit(solution)/shard_map/ppermute | solution.py:16
  20.9 5.4 %copy-start.7 = (s32[256]{0:T(256)S(1)}, s32[256]{0:T(256)}, u32[]{:S(2)}) copy-start(s32[256]{0:T(256)} %param.10) | copy-start | bytes 3076
  20.9 5.4 %copy-start.6 = (s32[256]{0:T(256)S(1)}, s32[256]{0:T(256)}, u32[]{:S(2)}) copy-start(s32[256]{0:T(256)} %param.11) | copy-start | bytes 3076
  20.9 94.4 %collective-permute-start = (f32[1,48,128]{2,1,0:T(8,128)S(1)}, f32[1,48,128]{2,1,0:T(8,128)S(1)}, u32[]{:S(2)}, u32[]{:S(2)}) collective-permute-start(f32[1,48,128]{2,1,0:T(8,128)S(1)} %get-tuple-element.24), channel_id=1, source_target_pairs={{1,0},{2,1},{3,2},{4,3},{5,4},{6,5},{7,6},{9,8},{10,9},{11,10},{12... | collective-permute-start | bytes 73736 | tf_op jit(solution)/shard_map/ppermute | solution.py:19
  22.4 93.0 %collective-permute-start.1 = (f32[1,48,128]{2,1,0:T(8,128)S(1)}, f32[1,48,128]{2,1,0:T(8,128)S(1)}, u32[]{:S(2)}, u32[]{:S(2)}) collective-permute-start(f32[1,48,128]{2,1,0:T(8,128)S(1)} %get-tuple-element.25), channel_id=1, source_target_pairs={{0,1},{1,2},{2,3},{3,4},{4,5},{5,6},{6,7},{8,9},{9,10},{10,11},{11... | collective-permute-start | bytes 73736 | tf_op jit(solution)/shard_map/ppermute | solution.py:16
  29.2 21.1 %copy-start.5 = (f32[32]{0:T(128)S(1)}, f32[32]{0:T(128)}, u32[]{:S(2)}) copy-start(f32[32]{0:T(128)} %param.14) | copy-start | bytes 388
  29.2 21.8 %copy-start.3 = (f32[3072]{0:T(1024)S(1)}, f32[3072]{0:T(1024)}, u32[]{:S(2)}) copy-start(f32[3072]{0:T(1024)} %param.16) | copy-start | bytes 36868
  29.2 38.4 %all-to-all-start = ((bf16[64,8,128]{2,1,0:T(8,128)(2,1)}), bf16[64,8,128]{2,1,0:T(8,128)(2,1)S(1)}, u32[]{:S(2)}, u32[]{:S(2)}) async-start(bf16[64,8,128]{2,1,0:T(8,128)(2,1)} %fusion.2), calls=%async_computation | async-start | bytes 262144 | tf_op jit(solution)/shard_map/all_to_all | solution.py:106
  50.3 2.9 copy-start.4
  55.5 0.7 copy-start.8
  67.8 0.8 copy-start.2
  68.8 46.5 %copy-start.1 = (f32[4,48,128]{2,1,0:T(8,128)S(1)}, f32[4,48,128]{2,1,0:T(8,128)}, u32[]{:S(2)}) copy-start(f32[4,48,128]{2,1,0:T(8,128)} %param.17) | copy-start | bytes 294916
  115.6 20.3 %collective-permute-start.4 = (f32[1,48,128]{2,1,0:T(8,128)S(1)}, f32[1,48,128]{2,1,0:T(8,128)S(1)}, u32[]{:S(2)}, u32[]{:S(2)}) collective-permute-start(f32[1,48,128]{2,1,0:T(8,128)S(1)} %get-tuple-element.20), channel_id=1, source_target_pairs={{1,0},{2,1},{3,2},{4,3},{5,4},{6,5},{7,6},{9,8},{10,9},{11,10},{12... | collective-permute-start | bytes 73736 | tf_op jit(solution)/shard_map/ppermute | solution.py:19
  116.9 19.0 %collective-permute-start.5 = (f32[1,48,128]{2,1,0:T(8,128)S(1)}, f32[1,48,128]{2,1,0:T(8,128)S(1)}, u32[]{:S(2)}, u32[]{:S(2)}) collective-permute-start(f32[1,48,128]{2,1,0:T(8,128)S(1)} %get-tuple-element.21), channel_id=1, source_target_pairs={{0,1},{1,2},{2,3},{3,4},{4,5},{5,6},{6,7},{8,9},{9,10},{10,11},{11... | collective-permute-start | bytes 73736 | tf_op jit(solution)/shard_map/ppermute | solution.py:16
  120.9 14.3 %collective-permute-start.6 = (f32[4,1,128]{2,1,0:T(1,128)S(1)}, f32[4,1,128]{2,1,0:T(1,128)S(1)}, u32[]{:S(2)}, u32[]{:S(2)}) collective-permute-start(f32[4,1,128]{2,1,0:T(1,128)S(1)} %get-tuple-element.22), channel_id=1, source_target_pairs={{8,0},{16,8},{24,16},{32,24},{40,32},{48,40},{56,48},{64,56},{72,6... | collective-permute-start | bytes 6152 | tf_op jit(solution)/shard_map/ppermute | solution.py:19
  128.8 7.1 %collective-permute-start.7 = (f32[4,1,128]{2,1,0:T(1,128)S(1)}, f32[4,1,128]{2,1,0:T(1,128)S(1)}, u32[]{:S(2)}, u32[]{:S(2)}) collective-permute-start(f32[4,1,128]{2,1,0:T(1,128)S(1)} %get-tuple-element.23), channel_id=1, source_target_pairs={{0,8},{8,16},{16,24},{24,32},{32,40},{40,48},{48,56},{56,64},{64,7... | collective-permute-start | bytes 6152 | tf_op jit(solution)/shard_map/ppermute | solution.py:16
  347.9 20.3 %collective-permute-start.8 = (f32[1,48,128]{2,1,0:T(8,128)S(1)}, f32[1,48,128]{2,1,0:T(8,128)S(1)}, u32[]{:S(2)}, u32[]{:S(2)}) collective-permute-start(f32[1,48,128]{2,1,0:T(8,128)S(1)} %get-tuple-element.16), channel_id=1, source_target_pairs={{1,0},{2,1},{3,2},{4,3},{5,4},{6,5},{7,6},{9,8},{10,9},{11,10},{12... | collective-permute-start | bytes 73736 | tf_op jit(solution)/shard_map/ppermute | solution.py:19
  349.2 19.0 %collective-permute-start.9 = (f32[1,48,128]{2,1,0:T(8,128)S(1)}, f32[1,48,128]{2,1,0:T(8,128)S(1)}, u32[]{:S(2)}, u32[]{:S(2)}) collective-permute-start(f32[1,48,128]{2,1,0:T(8,128)S(1)} %get-tuple-element.17), channel_id=1, source_target_pairs={{0,1},{1,2},{2,3},{3,4},{4,5},{5,6},{6,7},{8,9},{9,10},{10,11},{11... | collective-permute-start | bytes 73736 | tf_op jit(solution)/shard_map/ppermute | solution.py:16
  353.2 14.3 %collective-permute-start.10 = (f32[4,1,128]{2,1,0:T(1,128)S(1)}, f32[4,1,128]{2,1,0:T(1,128)S(1)}, u32[]{:S(2)}, u32[]{:S(2)}) collective-permute-start(f32[4,1,128]{2,1,0:T(1,128)S(1)} %get-tuple-element.18), channel_id=1, source_target_pairs={{8,0},{16,8},{24,16},{32,24},{40,32},{48,40},{56,48},{64,56},{72,6... | collective-permute-start | bytes 6152 | tf_op jit(solution)/shard_map/ppermute | solution.py:19
  356.3 11.9 %collective-permute-start.11 = (f32[4,1,128]{2,1,0:T(1,128)S(1)}, f32[4,1,128]{2,1,0:T(1,128)S(1)}, u32[]{:S(2)}, u32[]{:S(2)}) collective-permute-start(f32[4,1,128]{2,1,0:T(1,128)S(1)} %get-tuple-element.19), channel_id=1, source_target_pairs={{0,8},{8,16},{16,24},{24,32},{32,40},{40,48},{48,56},{56,64},{64,7... | collective-permute-start | bytes 6152 | tf_op jit(solution)/shard_map/ppermute | solution.py:16
where the time goes:
time: 480 us; the launch traced here: 478 us
  blocking collectives  362 us (75%)
  starting transfers between devices  84.4 us (18%)
  waiting for transfers between devices  12.7 us (3%)
  other arithmetic  7.66 us (2%)
  local copies, waits for them, and re-layouts  6.56 us (1%)
  between operations  5.05 us (1%)
    psum x2, blocking collectives, precond_total(): return lax.psum(jnp.sum(residual * precond), ('phi', 'row'))  208 us
    psum x1, blocking collectives, body(): alpha = norm_now / lax.psum(jnp.sum(direction * image), ('phi', 'row'))  107 us
    psum x1, blocking collectives, body(): boundary = lax.psum(partial_bnd, 'row')  46.3 us
    ppermute x6, starting transfers between devices, with_halo(): lax.ppermute(lax.slice_in_dim(block, block.shape[dim] - width, None, axis...  39.4 us
    ppermute x6, starting transfers between devices, with_halo(): lax.ppermute(lax.slice_in_dim(block, 0, width, axis=dim), axis, backward)  23.8 us
    all_to_all x1, starting transfers between devices, body(): lax.all_to_all(packed, 'phi', split_axis=0, concat_axis=0, tiled=True)  21.1 us
    all_to_all x1, waiting for transfers between devices, body(): lax.all_to_all(packed, 'phi', split_axis=0, concat_axis=0, tiled=True)  11.2 us
  transfers between devices with their start and end apart: 13, of which 3 were waited for; matrix products, arithmetic and copies ran while one was open for 2% of the time, Pallas kernels for 0%

commit v1 on v0

v1 whole, which is shorter than its diff:
```python
import functools

import jax
import jax.numpy as jnp
from jax import lax
from jax.experimental import pallas as pl
from jax.experimental.pallas import tpu as pltpu
from jax.sharding import PartitionSpec as P

MESH = pl.DeviceIdType.MESH
CAP = 8
PAD = 8
F32 = jnp.float32
BF16 = jnp.bfloat16
NT_DIMS = (((1,), (1,)), ((), ()))


def roll(x, shift, axis):
    return pltpu.roll(x, shift % x.shape[axis], axis)


def kernel(
    phis,
    rows,
    mag_ref,
    owner_ref,
    offset_ref,
    weight_ref,
    theta_ref,
    radial_ref,
    theta_coef_ref,
    phi_coef_ref,
    start_ref,
    x_out,
    r_out,
    pack,
    recv,
    wsend,
    wrecv,
    part,
    main,
    low,
    high,
    bound,
    field,
    inverse,
    base,
    sums,
    sums_plane,
    sums_column,
    pack_send,
    pack_recv,
    w_send,
    w_recv,
    part_send,
    main_recv,
    low_recv,
    high_recv,
    field_send,
    field_recv,
    plane_send,
    plane_recv,
    column_send,
    column_recv,
):
    phi = lax.axis_index("phi")
    row = lax.axis_index("row")
    planes = phis // 2
    column = 2 * rows
    cells = start_ref.shape[1]
    layers = start_ref.shape[0]
    width = start_ref.shape[2]
    half = lax.rem(lax.div(phi, 2), 2)
    other = 1 - half
    here = lax.div(phi, 4) * 2 + lax.rem(phi, 2)
    depth = half * rows + row
    slots = planes * 2 * CAP

    def phi_of(place, side):
        return lax.div(place, 2) * 4 + side * 2 + lax.rem(place, 2)

    partner = phi_of(here, other)

    def wrap(index):
        return lax.rem(index + phis, phis)

    up_phi = wrap(phi + 1)
    down_phi = wrap(phi - 1)

    barrier = pltpu.get_barrier_semaphore()

    def greet(device, level):
        pl.semaphore_signal(barrier, inc=1, device_id=(device, level), device_id_type=MESH)

    @pl.when(row == 0)
    def _():
        @pl.loop(0, column)
        def _(z):
            side, level = lax.div(z, rows), lax.rem(z, rows)
            for owner in (down_phi, up_phi):
                place = lax.div(owner, 4) * 2 + lax.rem(owner, 2)
                greet(phi_of(place, side), level)

    @pl.loop(0, column)
    def _(z):
        @pl.when(z != depth)
        def _():
            greet(phi_of(here, lax.div(z, rows)), lax.rem(z, rows))

    @pl.loop(0, planes)
    def _(place):
        @pl.when(place != here)
        def _():
            greet(phi_of(place, half), row)

    for near in (down_phi, up_phi):
        greet(near, row)

        @pl.when(row > 0)
        def _():
            greet(near, row - 1)

        @pl.when(row < rows - 1)
        def _():
            greet(near, row + 1)

    owner = owner_ref[...]
    target = (owner >> 2) * 32 + (owner & 1) * 16 + ((owner >> 1) & 1) * 8 + offset_ref[...]
    slot = lax.broadcasted_iota(jnp.int32, (slots, owner.shape[1]), 0)
    chosen = jnp.where(slot == target, 1.0, 0.0).astype(BF16)
    packed = jnp.dot(chosen, mag_ref[...], preferred_element_type=F32).astype(BF16)
    pack[...] = packed.reshape(planes, 2 * CAP, width)
    recv[here] = pack[here]

    weights = weight_ref[...]
    from_slot = lax.broadcasted_iota(jnp.int32, (slots, planes * CAP), 0)
    to_slot = lax.broadcasted_iota(jnp.int32, (slots, planes * CAP), 1)
    source = to_slot >> 3
    natural = ((source >> 1) * 4 + other * 2 + (source & 1)) * CAP + (to_slot & 7)
    pick = jnp.where(from_slot == natural, 1.0, 0.0).astype(BF16)
    wsend[...] = jnp.dot(weights, pick, preferred_element_type=F32).astype(BF16)

    for layer in range(layers):
        field[3 + layer, PAD : PAD + cells, :] = start_ref[layer]

    @pl.when(row == 0)
    def _():
        field[0:3] = jnp.zeros((3,) + field.shape[1:], F32)

    @pl.when(row == rows - 1)
    def _():
        field[3 + layers : 6 + layers] = jnp.zeros((3,) + field.shape[1:], F32)

    pl.semaphore_wait(
        barrier,
        (planes - 1)
        + (column - 1)
        + 4
        + 2
        * (
            1
            + jnp.where(row > 0, 1, 0).astype(jnp.int32)
            + jnp.where(row < rows - 1, 1, 0).astype(jnp.int32)
        ),
    )

    def remote(src, dst, send, receive, device, level):
        return pltpu.make_async_remote_copy(
            src_ref=src,
            dst_ref=dst,
            send_sem=send,
            recv_sem=receive,
            device_id=(device, level),
            device_id_type=MESH,
        )

    weight_copy = remote(
        wsend, wrecv, w_send, w_recv, partner, lax.rem(row + rows // 2, rows)
    )
    weight_copy.start()

    def pack_copy(place):
        return remote(
            pack.at[place],
            recv.at[here],
            pack_send.at[place],
            pack_recv.at[here],
            phi_of(place, half),
            row,
        )

    @pl.loop(0, planes)
    def _(place):
        @pl.when(place != here)
        def _():
            pack_copy(place).start()

    top, bottom = slice(layers - 3, layers), slice(0, 3)
    ghosts = []
    for side_index, (near, source_cells, ghost_cells) in enumerate(
        (
            (up_phi, slice(cells - PAD, cells), slice(0, PAD)),
            (down_phi, slice(0, PAD), slice(PAD + cells, 2 * PAD + cells)),
        )
    ):
        for kind, (step, source_layers, ghost_layers) in enumerate(
            (
                (0, slice(0, layers), slice(3, 3 + layers)),
                (1, slice(layers - 2, layers), slice(1, 3)),
                (-1, slice(0, 2), slice(3 + layers, 5 + layers)),
            )
        ):
            ghosts.append(
                (side_index * 3 + kind, near, step, source_layers, source_cells, ghost_layers, ghost_cells)
            )
    middle = slice(PAD, PAD + cells)
    ghosts.append((6, phi, 1, top, slice(0, cells), slice(0, 3), middle))
    ghosts.append((7, phi, -1, bottom, slice(0, cells), slice(3 + layers, 6 + layers), middle))

    def each_ghost(act, sending):
        for index, near, step, source_layers, source_cells, ghost_layers, ghost_cells in ghosts:
            copy = remote(
                start_ref.at[source_layers, source_cells],
                field.at[ghost_layers, ghost_cells],
                field_send.at[index],
                field_recv.at[index],
                near,
                row + step,
            )
            if step == 0:
                act(copy)
            else:
                exists = row < rows - 1 if (step > 0) == sending else row > 0

                @pl.when(exists)
                def _():
                    act(copy)

    each_ghost(lambda copy: copy.start(), True)

    tall = cells + 2 * PAD
    lanes = lax.broadcasted_iota(jnp.int32, (tall, width), 1)
    theta_coef = jnp.broadcast_to(theta_coef_ref[...], (tall, width))
    theta_upper = jnp.where(lanes < width - 1, 0.5 * (theta_coef + roll(theta_coef, -1, 1)), 0.0)
    theta_lower = jnp.where(lanes > 0, roll(theta_upper, 1, 1), 0.0)
    lines = phi_coef_ref.shape[0]
    first = lax.rem(phi * cells - PAD + lines * width, lines * width)
    line = lax.div(first, width)
    shift = width - lax.rem(first, width)
    near_line = phi_coef_ref[pl.ds(line, 1), :]
    next_line = phi_coef_ref[pl.ds(lax.rem(line + 1, lines), 1), :]
    lane8 = lax.broadcasted_iota(jnp.int32, (8, width), 1)
    window = jnp.where(
        lane8 < shift,
        pltpu.roll(jnp.broadcast_to(near_line, (8, width)), shift, 1),
        pltpu.roll(jnp.broadcast_to(next_line, (8, width)), shift, 1),
    )
    phi_face = 0.5 * (window + roll(window, -1, 1))
    phi_face = jnp.broadcast_to(phi_face[0:1], (width, width)).T
    phi_upper = phi_face[:tall]
    phi_lower = roll(phi_upper, 1, 0)
    top_index = layers * rows - 1

    def coef_at(index):
        return radial_ref[jnp.clip(index, 0, top_index)]

    radial_lower = [
        0.5 * (coef_at(row * layers + i - 4) + coef_at(row * layers + i - 3))
        for i in range(layers + 7)
    ]
    radial_upper = radial_lower[1:]
    around = phi_upper + phi_lower + theta_upper + theta_lower
    for i in range(1, layers + 5):
        index = row * layers + i - 3
        inside = jnp.where(jnp.logical_and(index >= 0, index <= top_index), 1.0, 0.0).astype(F32)
        inverse[i] = inside / (radial_upper[i] + radial_lower[i] + around)

    def image(values, i):
        value = values[i]
        result = radial_upper[i] * (value - values[i + 1])
        result = result + radial_lower[i] * (value - values[i - 1])
        result = result + theta_upper * (value - roll(value, -1, 1))
        result = result + theta_lower * (value - roll(value, 1, 1))
        result = result + phi_upper * (value - roll(value, -1, 0))
        return result + phi_lower * (value - roll(value, 1, 0))

    wide = (slots, slots)
    from_slot = lax.broadcasted_iota(jnp.int32, wide, 0)
    to_slot = lax.broadcasted_iota(jnp.int32, wide, 1)
    source = to_slot >> 4
    natural = ((source >> 1) * 4 + half * 2 + (source & 1)) * CAP + (to_slot & 7)
    mine = jnp.logical_and(from_slot == natural, ((to_slot >> 3) & 1) == half)
    own_weights = jnp.dot(
        weights, jnp.where(mine, 1.0, 0.0).astype(BF16), preferred_element_type=F32
    ).astype(BF16)
    from_slot = lax.broadcasted_iota(jnp.int32, (planes * CAP, slots), 0)
    to_slot = lax.broadcasted_iota(jnp.int32, (planes * CAP, slots), 1)
    theirs = jnp.logical_and(
        from_slot == (to_slot >> 4) * CAP + (to_slot & 7), ((to_slot >> 3) & 1) == other
    )
    theirs = jnp.where(theirs, 1.0, 0.0).astype(BF16)
    weight_copy.wait_recv()
    partner_weights = jnp.dot(wrecv[...], theirs, preferred_element_type=F32).astype(BF16)
    both_weights = jnp.concatenate([own_weights, partner_weights], axis=0)

    def pack_arrival(place):
        return remote(
            pack.at[place],
            recv.at[place],
            pack_send.at[place],
            pack_recv.at[place],
            phi_of(place, half),
            row,
        )

    @pl.loop(0, planes)
    def _(place):
        @pl.when(place != here)
        def _():
            pack_arrival(place).wait_recv()

    columns = jnp.dot(
        both_weights, recv[...].reshape(slots, width), preferred_element_type=F32
    )
    part[...] = jnp.dot(
        columns,
        theta_ref[...].astype(F32),
        preferred_element_type=F32,
        precision=lax.Precision.HIGHEST,
    )

    def part_copies():
        copies = []
        for index, owner in enumerate((phi, partner)):
            start = index * cells
            copies.append(
                remote(
                    part.at[start : start + PAD],
                    high.at[depth],
                    part_send.at[3 * index],
                    high_recv.at[depth],
                    wrap(owner - 1),
                    0,
                )
            )
            copies.append(
                remote(
                    part.at[start + cells - PAD : start + cells],
                    low.at[depth],
                    part_send.at[3 * index + 1],
                    low_recv.at[depth],
                    wrap(owner + 1),
                    0,
                )
            )
            copies.append(
                remote(
                    part.at[start : start + cells],
                    main.at[depth],
                    part_send.at[3 * index + 2],
                    main_recv.at[depth],
                    owner,
                    0,
                )
            )
        return copies

    part_list = part_copies()
    for index in (5, 3, 4, 0, 1):
        part_list[index].start()

    @pl.when(row > 0)
    def _():
        part_list[2].start()

    each_ghost(lambda copy: copy.wait_recv(), False)
    values = [field[i] for i in range(layers + 6)]
    for i in range(1, layers + 5):
        base[i] = -image(values, i)

    @pl.when(row == 0)
    def _():
        main[depth] = part[0:cells]

        @pl.loop(0, column)
        def _(z):
            def arrival(src, buffer, semaphore):
                return remote(
                    src, buffer.at[z], part_send.at[0], semaphore.at[z], phi, 0
                )

            arrival(part.at[0:PAD], low, low_recv).wait_recv()
            arrival(part.at[0:PAD], high, high_recv).wait_recv()

            @pl.when(z != depth)
            def _():
                arrival(part.at[0:cells], main, main_recv).wait_recv()

        bound[0:PAD] = jnp.sum(low[...], axis=0)
        bound[PAD : PAD + cells] = jnp.sum(main[...], axis=0)
        bound[PAD + cells :] = jnp.sum(high[...], axis=0)
        base[3] = base[3] + radial_lower[3] * bound[...]

    residual = {i: base[i] for i in range(1, layers + 5)}
    precond = {i: residual[i] * inverse[i] for i in range(1, layers + 5)}
    first_image = {i: image(precond, i) for i in range(2, layers + 4)}
    scaled = {i: first_image[i] * inverse[i] for i in range(2, layers + 4)}
    second_image = {i: image(scaled, i) for i in range(3, layers + 3)}

    def inner(left, right):
        total = 0.0
        for i in range(3, layers + 3):
            product = left[i] * right[i]
            for k in range(PAD, PAD + cells, 8):
                total = total + product[k : k + 8]
        return jnp.sum(jnp.sum(total, axis=0, keepdims=True), axis=1, keepdims=True)

    lane = lax.broadcasted_iota(jnp.int32, (1, width), 1)
    four = (
        inner(residual, precond),
        inner(precond, first_image),
        inner(first_image, scaled),
        inner(scaled, second_image),
    )
    packed_sums = jnp.zeros((1, width), F32)
    for index, value in enumerate(four):
        packed_sums = jnp.where(lane == index, value, packed_sums)
    sums[0] = packed_sums
    sums_plane[here] = packed_sums

    def plane_copy(place, slot):
        return remote(
            sums.at[0],
            sums_plane.at[slot],
            plane_send.at[place],
            plane_recv.at[slot],
            phi_of(place, half),
            row,
        )

    @pl.loop(0, planes)
    def _(place):
        @pl.when(place != here)
        def _():
            plane_copy(place, here).start()

    @pl.loop(0, planes)
    def _(place):
        @pl.when(place != here)
        def _():
            plane_copy(place, place).wait_recv()

    plane_sum = jnp.sum(sums_plane[...], axis=0)
    sums[1] = plane_sum
    sums_column[depth] = plane_sum

    def column_copy(z, slot):
        return remote(
            sums.at[1],
            sums_column.at[slot],
            column_send.at[z],
            column_recv.at[slot],
            phi_of(here, lax.div(z, rows)),
            lax.rem(z, rows),
        )

    @pl.loop(0, column)
    def _(z):
        @pl.when(z != depth)
        def _():
            column_copy(z, depth).start()

    @pl.loop(0, column)
    def _(z):
        @pl.when(z != depth)
        def _():
            column_copy(z, z).wait_recv()

    totals = jnp.sum(sums_column[...], axis=0)
    rz, pq, qw, wt = (
        jnp.sum(jnp.where(lane == index, totals, 0.0), axis=1, keepdims=True)
        for index in range(4)
    )
    step0 = rz / pq
    rz_next = step0 * step0 * qw - rz
    ratio = 1.0 + rz_next / rz
    step1 = rz_next / (step0 * step0 * wt - ratio * ratio * pq)
    along = step0 + step1 * ratio
    across = step0 * step1
    for layer in range(layers):
        i = 3 + layer
        part_of = slice(PAD, PAD + cells)
        x_out[layer] = (
            start_ref[layer] + along * precond[i][part_of] - across * scaled[i][part_of]
        )
        r_out[layer] = (
            residual[i][part_of]
            - along * first_image[i][part_of]
            + across * second_image[i][part_of]
        )

    weight_copy.wait_send()

    @pl.loop(0, planes)
    def _(place):
        @pl.when(place != here)
        def _():
            pack_copy(place).wait_send()
            plane_copy(place, here).wait_send()

    @pl.loop(0, column)
    def _(z):
        @pl.when(z != depth)
        def _():
            column_copy(z, depth).wait_send()

    each_ghost(lambda copy: copy.wait_send(), True)
    for index in (5, 3, 4, 0, 1):
        part_list[index].wait_send()

    @pl.when(row > 0)
    def _():
        part_list[2].wait_send()


def body(
    magnetogram,
    col_owner,
    col_offset,
    phi_weight,
    theta_weight,
    radial_coef,
    theta_coef,
    phi_coef,
    start_field,
):
    phis, rows = lax.axis_size("phi"), lax.axis_size("row")
    layers, cells, width = start_field.shape
    planes, column = phis // 2, 2 * rows
    slots = phis * CAP
    tall = cells + 2 * PAD
    dma = pltpu.SemaphoreType.DMA
    vmem = pl.BlockSpec(memory_space=pltpu.VMEM)
    in_specs = [vmem] * 9
    in_specs[5] = pl.BlockSpec(memory_space=pltpu.SMEM)
    shape = jax.ShapeDtypeStruct(start_field.shape, F32)
    return pl.pallas_call(
        functools.partial(kernel, phis, rows),
        out_shape=(shape, shape),
        in_specs=in_specs,
        out_specs=(vmem, vmem),
        scratch_shapes=[
            pltpu.VMEM((planes, 2 * CAP, width), BF16),
            pltpu.VMEM((planes, 2 * CAP, width), BF16),
            pltpu.VMEM((cells, planes * CAP), BF16),
            pltpu.VMEM((cells, planes * CAP), BF16),
            pltpu.VMEM((2 * cells, width), F32),
            pltpu.VMEM((column, cells, width), F32),
            pltpu.VMEM((column, PAD, width), F32),
            pltpu.VMEM((column, PAD, width), F32),
            pltpu.VMEM((tall, width), F32),
            pltpu.VMEM((layers + 6, tall, width), F32),
            pltpu.VMEM((layers + 6, tall, width), F32),
            pltpu.VMEM((layers + 6, tall, width), F32),
            pltpu.VMEM((2, 1, width), F32),
            pltpu.VMEM((planes, 1, width), F32),
            pltpu.VMEM((column, 1, width), F32),
            dma((planes,)),
            dma((planes,)),
            dma,
            dma,
            dma((6,)),
            dma((column,)),
            dma((column,)),
            dma((column,)),
            dma((8,)),
            dma((8,)),
            dma((planes,)),
            dma((planes,)),
            dma((column,)),
            dma((column,)),
        ],
        compiler_params=pltpu.CompilerParams(collective_id=0, has_side_effects=True),
    )(
        magnetogram,
        col_owner.reshape(1, -1),
        col_offset.reshape(1, -1),
        phi_weight.T,
        theta_weight,
        radial_coef,
        theta_coef.reshape(1, -1),
        phi_coef.reshape(-1, width),
        start_field,
    )


def solution(mesh):
    in_specs = (
        P("phi", "row"),
        P("phi"),
        P("phi"),
        P(None, "phi"),
        P("row", None),
        P(),
        P(),
        P(),
        P("row", "phi", None),
    )
    out_specs = (P("row", "phi", None), P("row", "phi", None))
    return jax.shard_map(body, mesh=mesh, in_specs=in_specs, out_specs=out_specs, check_vma=False)
```

time: 480 us -> 52.7 us (0.11)
  blocking collectives: 362 us -> 0 us
  starting transfers between devices: 84.4 us -> 0 us
  Pallas kernels: 0 us -> 49.7 us
  waiting for transfers between devices: 12.7 us -> 0 us
  other arithmetic: 7.66 us -> 0 us
    psum x4 -> x0, blocking collectives: 362 us -> none  [the longest x2 208 us: precond_total(): return lax.psum(jnp.sum(residual * precond), ('phi', 'row'))]
    ppermute x12 -> x0, starting transfers between devices: 63.3 us -> none  [the longest x6 39.4 us: with_halo(): lax.ppermute(lax.slice_in_dim(block, block.shape[dim] - width, None, axis...]
    pallas_call x0 -> x1, Pallas kernels: none -> 49.7 us  [body(): pl.pallas_call(functools.partial(kernel, phis, rows), out_shape=(shape, s...]
    all_to_all x1 -> x0, starting transfers between devices: 21.1 us -> none  [body(): lax.all_to_all(packed, 'phi', split_axis=0, concat_axis=0, tiled=True)]
    all_to_all x1 -> x0, waiting for transfers between devices: 11.2 us -> none  [body(): lax.all_to_all(packed, 'phi', split_axis=0, concat_axis=0, tiled=True)]
  transfers between devices with their start and end apart: 13 -> 0, of which waited for: 3 -> 0; matrix products, arithmetic and copies ran while one was open for 2% -> 0% of each run, Pallas kernels for 0% -> 0%
where the time goes in v1:
time: 52.7 us; the launch traced here: 52.5 us
  Pallas kernels  49.7 us (94%)
  local copies, waits for them, and re-layouts  2.22 us (4%)
  between operations  0.65 us (1%)
    pallas_call x1, Pallas kernels, body(): pl.pallas_call(functools.partial(kernel, phis, rows), out_shape=(shape, s...  49.7 us
    unnamed x4, local copies, waits for them, and re-layouts  2.22 us

profile of v1, /device:TPU:1, one launch (start us, length us, event | category | flops | bytes accessed | tf_op | source)
XLA Modules:
  0.0 52.5 jit_solution(16504603639092290059)
XLA Ops:
  0.6 49.7 %shard_map.104 = (f32[4,48,128]{2,1,0:T(8,128)}, f32[4,48,128]{2,1,0:T(8,128)}) custom-call(bf16[256,128]{1,0:T(8,128)(2,1)} %mag_ref.1, s32[1,256]{1,0:T(1,128)} %bitcast.7, s32[1,256]{1,0:T(1,128)} %bitcast.8, bf16[48,512]{1,0:T(8,128)(2,1)} %bitcast.5, bf16[128,128]{1,0:T(8,128)(2,1)} %theta_ref.1, f32[32]{0:T(128)} %radial_ref.1, f32[1,128]{1,0:T(1,128)} %bitcast.9, ...), custom_call_target="tpu_custom_call" | custom-call | tf_op jit(solution)/shard_map/pallas_call | solution.py:547
  50.3 0.0 copy-start
  50.3 1.6 %copy.13 = f32[4,48,128]{2,1,0:T(8,128)} copy(f32[4,48,128]{2,1,0:T(8,128)} %get-tuple-element.4) | data formatting | bytes 196608
  51.9 0.0 copy-done
  51.9 0.6 %copy.14 = f32[4,48,128]{2,1,0:T(8,128)} copy(f32[4,48,128]{2,1,0:T(8,128)S(1)} %copy-done) | data formatting | bytes 196608
Async XLA Ops:
  50.3 1.6 %copy-start = (f32[4,48,128]{2,1,0:T(8,128)S(1)}, f32[4,48,128]{2,1,0:T(8,128)}, u32[]{:S(2)}) copy-start(f32[4,48,128]{2,1,0:T(8,128)} %get-tuple-element.5) | copy-start | bytes 294916

commit v2 on v0

v2 whole, which is shorter than its diff:
```python
import functools

import jax
import jax.numpy as jnp
from jax import lax
from jax.experimental import pallas as pl
from jax.experimental.pallas import tpu as pltpu
from jax.sharding import PartitionSpec as P

MESH = pl.DeviceIdType.MESH
CAP = 8
PAD = 8
EDGE = 3
F32 = jnp.float32
BF16 = jnp.bfloat16


def roll(x, shift, axis):
    return pltpu.roll(x, shift % x.shape[axis], axis)


def kernel(
    phis,
    rows,
    mag_hbm,
    owner_hbm,
    offset_hbm,
    weight_hbm,
    theta_hbm,
    radial_hbm,
    theta_coef_hbm,
    phi_coef_hbm,
    start_hbm,
    fields_out,
    coef_out,
    mag_ref,
    owner_ref,
    offset_ref,
    weight_ref,
    theta_ref,
    radial_ref,
    theta_coef_ref,
    phi_coef_ref,
    pack,
    recv,
    wsend,
    wrecv,
    part,
    main,
    near_part,
    far_part,
    bound,
    forward,
    far_forward,
    mid,
    near_ghost,
    far_ghost,
    shadow_mid,
    shadow_near,
    field,
    inverse,
    faces,
    values,
    sums,
    sums_column,
    sums_plane,
    totals,
    in_sem,
    out_sem,
    pack_send,
    pack_recv,
    w_send,
    w_recv,
    part_send,
    main_recv,
    near_recv,
    far_recv,
    forward_send,
    forward_recv,
    radial_send,
    radial_recv,
    nghost_send,
    nghost_recv,
    fghost_send,
    fghost_recv,
    shadow_send,
    shadow_recv,
    column_send,
    column_recv,
    plane_send,
    plane_recv,
    total_send,
    total_recv,
):
    phi = lax.axis_index("phi")
    row = lax.axis_index("row")
    planes = phis // 2
    column = 2 * rows
    layers = start_hbm.shape[0]
    cells = start_hbm.shape[1]
    width = start_hbm.shape[2]
    tall = cells + 2 * PAD
    deep = layers + 2 * EDGE
    core = lax.rem(phi, 2)
    half = lax.rem(lax.div(phi, 2), 2)
    other = 1 - half
    here = lax.div(phi, 4) * 2 + core
    depth = half * rows + row
    slots = planes * 2 * CAP
    is_root = depth == 0
    is_second = depth == rows

    def phi_of(place, side):
        return lax.div(place, 2) * 4 + side * 2 + lax.rem(place, 2)

    def wrap(index):
        return lax.rem(index + phis, phis)

    def place_of(index):
        return lax.div(index, 4) * 2 + lax.rem(index, 2)

    twin = here + 1 - 2 * core
    near = phi + 1 - 2 * core
    far_step = 2 * core - 1
    far = wrap(phi + far_step)
    early_phi, late_phi = phi_of(here, 0), phi_of(here, 1)
    far_of_early, far_of_late = wrap(early_phi + far_step), wrap(late_phi + far_step)
    early_twin_phi = phi_of(twin, 0)
    last = cells - PAD
    near_src = pl.multiple_of((1 - core) * last, PAD)
    far_src = pl.multiple_of(core * last, PAD)

    inputs = [
        pltpu.make_async_copy(src, dst, in_sem.at[index])
        for index, (src, dst) in enumerate(
            (
                (owner_hbm, owner_ref),
                (offset_hbm, offset_ref),
                (mag_hbm, mag_ref),
                (weight_hbm, weight_ref),
                (start_hbm, mid.at[EDGE : EDGE + layers]),
                (radial_hbm, radial_ref),
                (theta_coef_hbm, theta_coef_ref),
                (phi_coef_hbm, phi_coef_ref),
                (theta_hbm, theta_ref),
            )
        )
    ]
    for copy in inputs:
        copy.start()

    has_next = row < rows - 1
    has_previous = row > 0

    def steps(act):
        act(0)

        @pl.when(has_next)
        def _():
            act(1)

        @pl.when(has_previous)
        def _():
            act(-1)

    barrier = pltpu.get_barrier_semaphore()

    def greet(device, level):
        pl.semaphore_signal(barrier, inc=1, device_id=(device, level), device_id_type=MESH)

    @pl.loop(1, planes)
    def _(step):
        greet(phi_of(lax.rem(here + step, planes), half), row)

    greet(phi_of(here, other), lax.rem(row + rows - rows // 2, rows))

    def greet_rows(step):
        if step != 0:
            greet(phi, row + step)
            greet(near, row + step)

    steps(greet_rows)

    @pl.when(half == 0)
    def _():
        steps(lambda step: greet(far, row + step))

    @pl.when(is_root)
    def _():
        @pl.loop(0, column)
        def _(z):
            side, level = lax.div(z, rows), lax.rem(z, rows)
            greet(phi_of(twin, side), level)
            greet(phi_of(place_of(far_of_early), side), level)

            @pl.when(z != 0)
            def _():
                greet(phi_of(here, side), level)

    for index in range(3):
        inputs[index].wait()
    owner = owner_ref[...]
    target = (owner >> 2) * 32 + (owner & 1) * 16 + ((owner >> 1) & 1) * 8 + offset_ref[...]
    slot = lax.broadcasted_iota(jnp.int32, (slots, owner.shape[1]), 0)
    chosen = jnp.where(slot == target, 1.0, 0.0).astype(BF16)
    packed = jnp.dot(chosen, mag_ref[...], preferred_element_type=F32).astype(BF16)
    pack[...] = packed.reshape(planes, 2 * CAP, width)
    recv[here] = pack[here]

    inputs[3].wait()
    weights = weight_ref[...]
    from_slot = lax.broadcasted_iota(jnp.int32, (slots, planes * CAP), 0)
    to_slot = lax.broadcasted_iota(jnp.int32, (slots, planes * CAP), 1)
    source = to_slot >> 3
    natural = ((source >> 1) * 4 + other * 2 + (source & 1)) * CAP + (to_slot & 7)
    pick = jnp.where(from_slot == natural, 1.0, 0.0).astype(BF16)
    wsend[...] = jnp.dot(weights, pick, preferred_element_type=F32).astype(BF16)
    inputs[4].wait()

    def flag(condition):
        return jnp.where(condition, 1, 0).astype(jnp.int32)

    pl.semaphore_wait(
        barrier,
        (planes - 1)
        + 1
        + 2 * (flag(has_next) + flag(has_previous))
        + half * (1 + flag(has_next) + flag(has_previous))
        + 2
        + flag(depth != 0),
    )

    def remote(src, dst, send, receive, device, level):
        return pltpu.make_async_remote_copy(
            src_ref=src,
            dst_ref=dst,
            send_sem=send,
            recv_sem=receive,
            device_id=(device, level),
            device_id_type=MESH,
        )

    weight_copy = remote(
        wsend, wrecv, w_send, w_recv, phi_of(here, other), lax.rem(row + rows // 2, rows)
    )
    weight_copy.start()

    def pack_copy(place, slot):
        return remote(
            pack.at[place],
            recv.at[slot],
            pack_send.at[place],
            pack_recv.at[slot],
            phi_of(place, half),
            row,
        )

    @pl.loop(1, planes)
    def _(step):
        pack_copy(lax.rem(here + step, planes), here).start()

    def layers_of(step):
        if step == 0:
            return pl.ds(EDGE, layers), pl.ds(EDGE, layers)
        if step > 0:
            return pl.ds(layers, EDGE), pl.ds(0, EDGE)
        return pl.ds(EDGE, EDGE), pl.ds(EDGE + layers, EDGE)

    def radial_copy(step):
        source, ghost = layers_of(step)
        return remote(
            mid.at[source],
            mid.at[ghost],
            radial_send.at[1 + step],
            radial_recv.at[1 - step],
            phi,
            row + step,
        )

    def near_copy(step):
        source, ghost = layers_of(step)
        return remote(
            mid.at[source, pl.ds(near_src, PAD)],
            near_ghost.at[ghost],
            nghost_send.at[1 + step],
            nghost_recv.at[1 - step],
            near,
            row + step,
        )

    def far_copy(step):
        source, ghost = layers_of(step)
        return remote(
            mid.at[source, pl.ds(far_src, PAD)],
            far_ghost.at[ghost],
            fghost_send.at[1 + step],
            fghost_recv.at[1 - step],
            far,
            row + step,
        )

    def arrival(buffer, semaphore, step):
        _, ghost = layers_of(-step)
        return remote(
            buffer.at[ghost], buffer.at[ghost], w_send, semaphore.at[1 + step], near, row
        )

    def shadow_copies(step):
        if step == 0:
            source, ghost = pl.ds(EDGE, layers), pl.ds(EDGE, layers)
        else:
            source, ghost = pl.ds(EDGE, EDGE), pl.ds(EDGE + layers, EDGE)
        return (
            remote(
                mid.at[source],
                shadow_mid.at[ghost],
                shadow_send.at[0],
                shadow_recv.at[2 * step],
                early_phi,
                0,
            ),
            remote(
                mid.at[source, pl.ds(near_src, PAD)],
                shadow_near.at[ghost],
                shadow_send.at[1],
                shadow_recv.at[2 * step + 1],
                early_twin_phi,
                0,
            ),
        )

    def shadow_do(act):
        for step in (0, 1):

            @pl.when(depth == rows + step)
            def _():
                for copy in shadow_copies(step):
                    act(copy)

    @pl.when(half == 1)
    def _():
        steps(lambda step: far_copy(step).start())

    shadow_do(lambda copy: copy.start())

    def row_copies(step):
        if step != 0:
            radial_copy(step).start()
        near_copy(step).start()

    steps(row_copies)

    for index in range(5, 9):
        inputs[index].wait()
    lanes = lax.broadcasted_iota(jnp.int32, (tall, width), 1)
    theta_coef = jnp.broadcast_to(theta_coef_ref[...], (tall, width))
    theta_upper = jnp.where(lanes < width - 1, 0.5 * (theta_coef + roll(theta_coef, -1, 1)), 0.0)
    theta_lower = jnp.where(lanes > 0, roll(theta_upper, 1, 1), 0.0)
    lines = phi_coef_ref.shape[0]
    lane8 = lax.broadcasted_iota(jnp.int32, (8, width), 1)
    top_index = layers * rows - 1

    def radial_faces(level):
        def coef_at(index):
            return radial_ref[jnp.clip(index, 0, top_index)]

        return [
            0.5
            * (
                coef_at(level * layers + i - EDGE - 1)
                + coef_at(level * layers + i - EDGE)
            )
            for i in range(deep + 1)
        ]

    def inside(level, i):
        index = level * layers + i - EDGE
        return jnp.logical_and(index >= 0, index <= top_index)

    def set_faces(which, slab, level):
        first = lax.rem(slab * cells - PAD + lines * width, lines * width)
        line = lax.div(first, width)
        shift = width - lax.rem(first, width)
        near_line = phi_coef_ref[pl.ds(line, 1), :]
        next_line = phi_coef_ref[pl.ds(lax.rem(line + 1, lines), 1), :]
        window = jnp.where(
            lane8 < shift,
            pltpu.roll(jnp.broadcast_to(near_line, (8, width)), shift, 1),
            pltpu.roll(jnp.broadcast_to(next_line, (8, width)), shift, 1),
        )
        phi_face = 0.5 * (window + roll(window, -1, 1))
        phi_upper = jnp.broadcast_to(phi_face[0:1], (width, width)).T[:tall]
        phi_lower = roll(phi_upper, 1, 0)
        faces[which, 0] = phi_upper
        faces[which, 1] = phi_lower
        radial = radial_faces(level)
        around = phi_upper + phi_lower + theta_upper + theta_lower
        for i in range(1, deep - 1):
            weight = jnp.where(inside(level, i), 1.0, 0.0).astype(F32)
            inverse[which, i] = weight / (radial[i] + radial[i + 1] + around)

    def image(which, radial, cell, i):
        phi_upper, phi_lower = faces[which, 0], faces[which, 1]
        value = cell(i)
        result = radial[i + 1] * (value - cell(i + 1))
        result = result + radial[i] * (value - cell(i - 1))
        result = result + theta_upper * (value - roll(value, -1, 1))
        result = result + theta_lower * (value - roll(value, 1, 1))
        result = result + phi_upper * (value - roll(value, -1, 0))
        return result + phi_lower * (value - roll(value, 1, 0))

    def at(which, kind):
        return lambda i: values[which, kind, i]

    def evaluate(which, level):
        radial = radial_faces(level)
        for i in range(1, deep - 1):
            residual = -image(which, radial, lambda j: field[which, j], i)
            values[which, 0, i] = residual
            values[which, 1, i] = residual * inverse[which, i]
        for i in range(2, deep - 2):
            first = image(which, radial, at(which, 1), i)
            values[which, 2, i] = first
            values[which, 3, i] = first * inverse[which, i]
        for i in range(3, deep - 3):
            values[which, 4, i] = image(which, radial, at(which, 3), i)

    def add_boundary(which, boundary):
        radial = radial_faces(0)
        residual = values[which, 0, EDGE] + radial[EDGE] * boundary
        values[which, 0, EDGE] = residual
        values[which, 1, EDGE] = residual * inverse[which, EDGE]
        for i in (EDGE, EDGE + 1):
            first = image(which, radial, at(which, 1), i)
            values[which, 2, i] = first
            values[which, 3, i] = first * inverse[which, i]
        for i in (EDGE, EDGE + 1, EDGE + 2):
            values[which, 4, i] = image(which, radial, at(which, 3), i)

    cell_index = lax.broadcasted_iota(jnp.int32, (tall, width), 0)
    lane = lax.broadcasted_iota(jnp.int32, (1, width), 1)

    def inner_sums(which, side):
        reach = EDGE * (1 - 2 * side)
        low = PAD - (1 - core) * reach
        high = PAD + cells + core * reach
        counted = jnp.logical_and(cell_index >= low, cell_index < high)
        result = jnp.zeros((1, width), F32)
        for index, (left, right) in enumerate(((0, 1), (1, 2), (2, 3), (3, 4))):
            total = None
            for i in range(EDGE, EDGE + layers):
                product = values[which, left, i] * values[which, right, i]
                total = product if total is None else total + product
            total = jnp.where(counted, total, 0.0)
            total = jnp.sum(total, axis=0, keepdims=True)
            total = jnp.sum(total, axis=1, keepdims=True)
            result = jnp.where(lane == index, total, result)
        return result

    def assemble(which, middle, near_cells, far_cells, level):
        for i in range(deep):
            keep = inside(level, i)
            near_value = jnp.where(keep, near_cells[i], 0.0)
            far_value = jnp.zeros_like(near_value)
            if far_cells is not None:
                far_value = jnp.where(keep, far_cells[i], 0.0)
            field[which, i, 0:PAD] = jnp.where(core == 0, far_value, near_value)
            field[which, i, PAD + cells : tall] = jnp.where(core == 0, near_value, far_value)
            field[which, i, PAD : PAD + cells] = jnp.where(keep, middle[i], 0.0)

    set_faces(0, phi, row)

    wide = (slots, slots)
    from_slot = lax.broadcasted_iota(jnp.int32, wide, 0)
    to_slot = lax.broadcasted_iota(jnp.int32, wide, 1)
    source = to_slot >> 4
    natural = ((source >> 1) * 4 + half * 2 + (source & 1)) * CAP + (to_slot & 7)
    mine = jnp.logical_and(from_slot == natural, ((to_slot >> 3) & 1) == half)
    own_weights = jnp.dot(
        weights, jnp.where(mine, 1.0, 0.0).astype(BF16), preferred_element_type=F32
    )
    from_slot = lax.broadcasted_iota(jnp.int32, (planes * CAP, slots), 0)
    to_slot = lax.broadcasted_iota(jnp.int32, (planes * CAP, slots), 1)
    theirs = jnp.logical_and(
        from_slot == (to_slot >> 4) * CAP + (to_slot & 7), ((to_slot >> 3) & 1) == other
    )
    theirs = jnp.where(theirs, 1.0, 0.0).astype(BF16)
    theta = theta_ref[...].astype(F32)
    weight_copy.wait_recv()
    partner_weights = jnp.dot(wrecv[...], theirs, preferred_element_type=F32)
    both_weights = jnp.concatenate(
        [
            jnp.where(half == 0, own_weights, partner_weights),
            jnp.where(half == 0, partner_weights, own_weights),
        ],
        axis=0,
    ).astype(BF16)

    @pl.loop(1, planes)
    def _(step):
        place = lax.rem(here + step, planes)
        pack_copy(place, place).wait_recv()

    columns = jnp.dot(
        both_weights, recv[...].reshape(slots, width), preferred_element_type=F32
    )
    product = jnp.dot(
        columns, theta, preferred_element_type=F32, precision=lax.Precision.HIGHEST
    )
    part[...] = product.reshape(2, cells, width)

    main_copy = remote(part, main.at[depth], part_send.at[0], main_recv.at[depth], early_phi, 0)
    near_part_copy = remote(
        part.at[:, pl.ds(near_src, PAD)],
        near_part.at[depth],
        part_send.at[1],
        near_recv.at[depth],
        early_twin_phi,
        0,
    )
    far_part_copy = remote(
        part.at[1, pl.ds(far_src, PAD)],
        far_part.at[depth],
        part_send.at[2],
        far_recv.at[depth],
        far_of_late,
        0,
    )
    far_part_copy.start()
    near_part_copy.start()

    @pl.when(depth != 0)
    def _():
        main_copy.start()

    def wait_rows(step):
        if step != 0:
            arrival(mid, radial_recv, step).wait_recv()
        arrival(near_ghost, nghost_recv, step).wait_recv()

    steps(wait_rows)

    @pl.when(half == 0)
    def _():
        def back(step):
            arrival(far_ghost, fghost_recv, step).wait_recv()
            far_copy(step).start()

        steps(back)
        assemble(0, mid, near_ghost, far_ghost, row)

    @pl.when(half == 1)
    def _():
        assemble(0, mid, near_ghost, None, row)

    evaluate(0, row)

    column_copy = remote(
        sums.at[0], sums_column.at[depth], column_send, column_recv.at[depth], early_phi, 0
    )

    @pl.when(depth != 0)
    def _():
        own = inner_sums(0, half)
        sums[0] = jnp.where(is_second, 0.0, own)
        column_copy.start()

    def total_copy(z):
        return remote(
            totals,
            totals,
            total_send.at[z],
            total_recv,
            phi_of(here, lax.div(z, rows)),
            lax.rem(z, rows),
        )

    def plane_copy(place, slot):
        return remote(
            sums.at[1],
            sums_plane.at[slot],
            plane_send.at[place],
            plane_recv.at[slot],
            phi_of(place, 0),
            0,
        )

    forward_copy = remote(
        bound.at[1], forward, forward_send.at[0], forward_recv.at[0], late_phi, 0
    )
    far_forward_copy = remote(
        bound.at[0, pl.ds(pl.multiple_of(PAD + far_src, PAD), PAD)],
        far_forward,
        forward_send.at[1],
        forward_recv.at[1],
        far_of_early,
        0,
    )

    def send_fields():
        copy = pltpu.make_async_copy(
            values.at[0, :, EDGE : EDGE + layers, PAD : PAD + cells], fields_out, out_sem.at[0]
        )
        return copy

    def sides(near_value, far_value):
        return (
            jnp.where(core == 0, far_value, near_value),
            jnp.where(core == 0, near_value, far_value),
        )

    @pl.when(is_root)
    def _():
        set_faces(1, late_phi, 0)
        for step in (0, 1):
            for copy in shadow_copies(step):
                copy.wait_recv()
        assemble(1, shadow_mid, shadow_near, None, 0)
        evaluate(1, 0)
        main[0] = part[...]

        @pl.loop(1, column)
        def _(z):
            remote(
                sums.at[0], sums_column.at[z], column_send, column_recv.at[z], phi, 0
            ).wait_recv()

        @pl.loop(0, column)
        def _(z):
            remote(
                near_part.at[z], near_part.at[z], part_send.at[1], near_recv.at[z], phi, 0
            ).wait_recv()
            remote(
                far_part.at[z], far_part.at[z], part_send.at[2], far_recv.at[z], phi, 0
            ).wait_recv()

            @pl.when(z != 0)
            def _():
                remote(part, main.at[z], part_send.at[0], main_recv.at[z], phi, 0).wait_recv()

        middle = jnp.sum(main[...], axis=0)
        nears = jnp.sum(near_part[...], axis=0)
        fars = jnp.sum(far_part[...], axis=0)
        for which in (0, 1):
            low, high = sides(nears[which], fars if which == 0 else jnp.zeros_like(fars))
            bound[which, 0:PAD] = low
            bound[which, PAD : PAD + cells] = middle[which]
            bound[which, PAD + cells : tall] = high
            add_boundary(which, bound[which])
        sums_column[0] = inner_sums(0, 0) + inner_sums(1, 1)
        mine = jnp.sum(sums_column[...], axis=0)
        sums[1] = mine
        sums_plane[here] = mine

        @pl.loop(1, planes)
        def _(step):
            plane_copy(lax.rem(here + step, planes), here).start()

        forward_copy.start()
        far_forward_copy.start()
        send_fields().start()

        @pl.loop(1, planes)
        def _(step):
            place = lax.rem(here + step, planes)
            plane_copy(place, place).wait_recv()

        totals[...] = jnp.sum(sums_plane[...], axis=0)

        @pl.loop(1, column)
        def _(z):
            total_copy(z).start()

    @pl.when(half == 1)
    def _():
        steps(lambda step: arrival(far_ghost, fghost_recv, step).wait_recv())
        assemble(0, mid, near_ghost, far_ghost, row)
        evaluate(0, row)

    @pl.when(is_second)
    def _():
        forward_copy.wait_recv()
        far_forward_copy.wait_recv()
        boundary = forward[...]
        edge = jnp.where(core == 0, far_forward[...], boundary[0:PAD])
        other_edge = jnp.where(core == 0, boundary[PAD + cells :], far_forward[...])
        add_boundary(
            0, jnp.concatenate([edge, boundary[PAD : PAD + cells], other_edge], axis=0)
        )

    @pl.when(depth != 0)
    def _():
        send_fields().start()
        remote(totals, totals, total_send.at[0], total_recv, phi, 0).wait_recv()

    total = totals[...]
    rz, pq, qw, wt = (
        jnp.sum(jnp.where(lane == index, total, 0.0), axis=1, keepdims=True)
        for index in range(4)
    )
    step0 = rz / pq
    rz_next = step0 * step0 * qw - rz
    ratio = 1.0 + rz_next / rz
    step1 = rz_next / (step0 * step0 * wt - ratio * ratio * pq)
    along = step0 + step1 * ratio
    across = step0 * step1
    coef_out[0:1] = jnp.broadcast_to(along, (1, width))
    coef_out[1:2] = jnp.broadcast_to(across, (1, width))

    send_fields().wait()
    weight_copy.wait_send()

    @pl.loop(1, planes)
    def _(step):
        pack_copy(lax.rem(here + step, planes), here).wait_send()

    def sent_rows(step):
        if step != 0:
            radial_copy(step).wait_send()
        near_copy(step).wait_send()
        far_copy(step).wait_send()

    steps(sent_rows)
    shadow_do(lambda copy: copy.wait_send())
    near_part_copy.wait_send()
    far_part_copy.wait_send()

    @pl.when(depth != 0)
    def _():
        main_copy.wait_send()
        column_copy.wait_send()

    @pl.when(is_root)
    def _():
        forward_copy.wait_send()
        far_forward_copy.wait_send()

        @pl.loop(1, planes)
        def _(step):
            plane_copy(lax.rem(here + step, planes), here).wait_send()

        @pl.loop(1, column)
        def _(z):
            total_copy(z).wait_send()


def body(
    magnetogram,
    col_owner,
    col_offset,
    phi_weight,
    theta_weight,
    radial_coef,
    theta_coef,
    phi_coef,
    start_field,
):
    phis, rows = lax.axis_size("phi"), lax.axis_size("row")
    layers, cells, width = start_field.shape
    planes, column = phis // 2, 2 * rows
    slots = phis * CAP
    tall = cells + 2 * PAD
    deep = layers + 2 * EDGE
    dma = pltpu.SemaphoreType.DMA
    anywhere = pl.BlockSpec(memory_space=pl.ANY)
    operands = (
        magnetogram,
        col_owner.reshape(1, -1),
        col_offset.reshape(1, -1),
        phi_weight.T,
        theta_weight,
        radial_coef,
        theta_coef.reshape(1, -1),
        phi_coef.reshape(-1, width),
        start_field,
    )
    local = [pltpu.VMEM(x.shape, x.dtype) for x in operands[:8]]
    local[5] = pltpu.SMEM(radial_coef.shape, F32)
    fields, coef = pl.pallas_call(
        functools.partial(kernel, phis, rows),
        out_shape=(
            jax.ShapeDtypeStruct((5,) + start_field.shape, F32),
            jax.ShapeDtypeStruct((2, width), F32),
        ),
        in_specs=[anywhere] * 9,
        out_specs=(anywhere, pl.BlockSpec(memory_space=pltpu.VMEM)),
        scratch_shapes=local
        + [
            pltpu.VMEM((planes, 2 * CAP, width), BF16),
            pltpu.VMEM((planes, 2 * CAP, width), BF16),
            pltpu.VMEM((cells, planes * CAP), BF16),
            pltpu.VMEM((cells, planes * CAP), BF16),
            pltpu.VMEM((2, cells, width), F32),
            pltpu.VMEM((column, 2, cells, width), F32),
            pltpu.VMEM((column, 2, PAD, width), F32),
            pltpu.VMEM((column, PAD, width), F32),
            pltpu.VMEM((2, tall, width), F32),
            pltpu.VMEM((tall, width), F32),
            pltpu.VMEM((PAD, width), F32),
            pltpu.VMEM((deep, cells, width), F32),
            pltpu.VMEM((deep, PAD, width), F32),
            pltpu.VMEM((deep, PAD, width), F32),
            pltpu.VMEM((deep, cells, width), F32),
            pltpu.VMEM((deep, PAD, width), F32),
            pltpu.VMEM((2, deep, tall, width), F32),
            pltpu.VMEM((2, deep, tall, width), F32),
            pltpu.VMEM((2, 2, tall, width), F32),
            pltpu.VMEM((2, 5, deep, tall, width), F32),
            pltpu.VMEM((2, 1, width), F32),
            pltpu.VMEM((column, 1, width), F32),
            pltpu.VMEM((planes, 1, width), F32),
            pltpu.VMEM((1, width), F32),
            dma((9,)),
            dma((1,)),
            dma((planes,)),
            dma((planes,)),
            dma,
            dma,
            dma((3,)),
            dma((column,)),
            dma((column,)),
            dma((column,)),
            dma((2,)),
            dma((2,)),
            dma((3,)),
            dma((3,)),
            dma((3,)),
            dma((3,)),
            dma((3,)),
            dma((3,)),
            dma((2,)),
            dma((4,)),
            dma,
            dma((column,)),
            dma((planes,)),
            dma((planes,)),
            dma((column,)),
            dma,
        ],
        compiler_params=pltpu.CompilerParams(collective_id=0, has_side_effects=True),
    )(*operands)
    along, across = coef[0], coef[1]
    solution_field = start_field + along * fields[1] - across * fields[3]
    residual = fields[0] - along * fields[2] + across * fields[4]
    return solution_field, residual


def solution(mesh):
    in_specs = (
        P("phi", "row"),
        P("phi"),
        P("phi"),
        P(None, "phi"),
        P("row", None),
        P(),
        P(),
        P(),
        P("row", "phi", None),
    )
    out_specs = (P("row", "phi", None), P("row", "phi", None))
    return jax.shard_map(body, mesh=mesh, in_specs=in_specs, out_specs=out_specs, check_vma=False)
```

time: 480 us -> 58.3 us (0.12)
  blocking collectives: 362 us -> 0 us
  starting transfers between devices: 84.4 us -> 0 us
  Pallas kernels: 0 us -> 55 us
  waiting for transfers between devices: 12.7 us -> 0 us
  local copies, waits for them, and re-layouts: 6.56 us -> 0.63 us
  other arithmetic: 7.66 us -> 1.79 us
    psum x4 -> x0, blocking collectives: 362 us -> none  [the longest x2 208 us: precond_total(): return lax.psum(jnp.sum(residual * precond), ('phi', 'row'))]
    ppermute x12 -> x0, starting transfers between devices: 63.3 us -> none  [the longest x6 39.4 us: with_halo(): lax.ppermute(lax.slice_in_dim(block, block.shape[dim] - width, None, axis...]
    pallas_call x0 -> x1, Pallas kernels: none -> 55 us  [body(): pl.pallas_call(functools.partial(kernel, phis, rows), out_shape=(jax.Shap...]
    all_to_all x1 -> x0, starting transfers between devices: 21.1 us -> none  [body(): lax.all_to_all(packed, 'phi', split_axis=0, concat_axis=0, tiled=True)]
    all_to_all x1 -> x0, waiting for transfers between devices: 11.2 us -> none  [body(): lax.all_to_all(packed, 'phi', split_axis=0, concat_axis=0, tiled=True)]
  transfers between devices with their start and end apart: 13 -> 0, of which waited for: 3 -> 0; matrix products, arithmetic and copies ran while one was open for 2% -> 0% of each run, Pallas kernels for 0% -> 0%
where the time goes in v2:
time: 58.3 us; the launch traced here: 58.1 us
  Pallas kernels  55 us (94%)
  other arithmetic  1.79 us (3%)
  between operations  0.66 us (1%)
  local copies, waits for them, and re-layouts  0.63 us (1%)
    pallas_call x1, Pallas kernels, body(): pl.pallas_call(functools.partial(kernel, phis, rows), out_shape=(jax.Shap...  55 us
    add x1, other arithmetic, body(): residual = fields[0] - along * fields[2] + across * fields[4]  1.79 us

profile of v2, /device:TPU:1, one launch (start us, length us, event | category | flops | bytes accessed | tf_op | source)
XLA Modules:
  0.0 58.1 jit_solution(27142173843304934)
XLA Ops:
  0.6 0.0 copy-start
  0.6 55.0 %shard_map.104 = (f32[5,4,48,128]{3,2,1,0:T(8,128)}, f32[2,128]{1,0:T(2,128)}) custom-call(bf16[256,128]{1,0:T(8,128)(2,1)} %mag_hbm.1, s32[1,256]{1,0:T(1,128)} %bitcast.33, s32[1,256]{1,0:T(1,128)} %bitcast.34, bf16[48,512]{1,0:T(8,128)(2,1)} %bitcast.31, bf16[128,128]{1,0:T(8,128)(2,1)} %theta_hbm.1, f32[32]{0:T(128)} %radial_hbm.1, f32[1,128]{1,0:T(1,128)} %bitcast.35, ...), custom_call_target="tpu_custom_call" | custom-call | tf_op jit(solution)/shard_map/pallas_call | solution.py:779
  55.6 0.0 copy-start.1
  55.6 0.6 %copy-done.1 = f32[2,128]{1,0:T(2,128)S(1)} copy-done((f32[2,128]{1,0:T(2,128)S(1)}, f32[2,128]{1,0:T(2,128)}, u32[]{:S(2)}) %copy-start.1) | copy-done | bytes 1048
  56.3 0.0 copy-done
  56.3 1.8 %fusion = (f32[4,48,128]{2,1,0:T(8,128)}, f32[4,48,128]{2,1,0:T(8,128)}) fusion(f32[5,4,48,128]{3,2,1,0:T(8,128)} %get-tuple-element.5, f32[128]{0:T(128)S(1)} %get-tuple-element.9, f32[128]{0:T(128)S(1)} %get-tuple-element.8, f32[4,48,128]{2,1,0:T(8,128)S(1)} %copy-done), kind=kLoop, calls=%fused_computation.1 | loop fusion | flops 196608 | bytes 787456 | tf_op jit(solution)/shard_map/add | solution.py:844
  (1 shorter events, 0.0 us)
Async XLA Ops:
  0.6 55.6 %copy-start = (f32[4,48,128]{2,1,0:T(8,128)S(1)}, f32[4,48,128]{2,1,0:T(8,128)}, u32[]{:S(2)}) copy-start(f32[4,48,128]{2,1,0:T(8,128)} %start_hbm.1) | copy-start | bytes 294916
  55.6 0.6 %copy-start.1 = (f32[2,128]{1,0:T(2,128)S(1)}, f32[2,128]{1,0:T(2,128)}, u32[]{:S(2)}) copy-start(f32[2,128]{1,0:T(2,128)} %get-tuple-element.4) | copy-start | bytes 3076

commit v3 on v2

--- a/solution.py
+++ b/solution.py
@@ -66,7 +66,6 @@
     sums_plane,
     totals,
     in_sem,
-    out_sem,
     pack_send,
     pack_recv,
     w_send,
@@ -110,6 +109,42 @@
     is_root = depth == 0
     is_second = depth == rows
 
+    offsets = (1, 2, 4)
+    reach = jnp.where(half == 0, row, column - depth)
+    bit = jnp.where(
+        lax.rem(reach, 2) == 1, 1, jnp.where(lax.rem(reach, 4) == 2, 2, 4)
+    ).astype(jnp.int32)
+    bit = jnp.where(reach == rows, 2, bit).astype(jnp.int32)
+    parent_reach = jnp.where(reach == rows, rows - 2, reach - bit).astype(jnp.int32)
+    is_feeder = jnp.logical_and(parent_reach == 0, depth != 0)
+    parent_half = jnp.where(parent_reach == 0, 0, half).astype(jnp.int32)
+    parent_depth = jnp.where(half == 0, parent_reach, column - parent_reach)
+    parent_depth = jnp.where(parent_reach == 0, 0, parent_depth).astype(jnp.int32)
+    parent_row = parent_depth - parent_half * rows
+    tree_slot = lax.div(bit, 2) + jnp.where(is_feeder, 3 * half, 0).astype(jnp.int32)
+    inner = jnp.logical_and(reach > 0, reach < rows)
+    has_child = (
+        jnp.logical_and(inner, jnp.logical_and(lax.rem(reach, 2) == 0, reach + 1 < rows)),
+        jnp.logical_and(
+            inner,
+            jnp.logical_or(
+                jnp.logical_and(lax.rem(reach, 4) == 0, reach + 2 < rows),
+                jnp.logical_and(half == 1, reach == rows - 2),
+            ),
+        ),
+    )
+    child_depth = [
+        jnp.where(half == 0, depth + offset, depth - offset).astype(jnp.int32)
+        for offset in offsets[:2]
+    ]
+    feeders = [(0, 0)]
+    for index, offset in enumerate(offsets):
+        if offset < rows:
+            feeders += [(offset, 1 + index), (column - offset, 4 + index)]
+        elif offset == rows == 2:
+            feeders.append((column - offset, 4 + index))
+    feeder_slot = jnp.where(is_feeder, 1 + tree_slot, 0).astype(jnp.int32)
+
     def phi_of(place, side):
         return lax.div(place, 2) * 4 + side * 2 + lax.rem(place, 2)
 
@@ -187,15 +222,23 @@
 
     @pl.when(is_root)
     def _():
-        @pl.loop(0, column)
-        def _(z):
-            side, level = lax.div(z, rows), lax.rem(z, rows)
+        for z, _slot in feeders:
+            side, level = z // rows, z % rows
             greet(phi_of(twin, side), level)
             greet(phi_of(place_of(far_of_early), side), level)
 
-            @pl.when(z != 0)
-            def _():
-                greet(phi_of(here, side), level)
+        for step in (0, 1):
+            greet(phi_of(twin, 1), step)
+
+        @pl.loop(1, column)
+        def _(z):
+            greet(phi_of(here, lax.div(z, rows)), lax.rem(z, rows))
+
+    for index in range(2):
+
+        @pl.when(has_child[index])
+        def _():
+            greet(phi, child_depth[index] - half * rows)
 
     for index in range(3):
         inputs[index].wait()
@@ -226,8 +269,10 @@
         + 1
         + 2 * (flag(has_next) + flag(has_previous))
         + half * (1 + flag(has_next) + flag(has_previous))
-        + 2
-        + flag(depth != 0),
+        + flag(depth != 0)
+        + 2 * flag(jnp.logical_or(is_feeder, is_root))
+        + flag(jnp.logical_and(depth != 0, parent_reach != 0))
+        + flag(jnp.logical_or(depth == rows, depth == rows + 1)),
     )
 
     def remote(src, dst, send, receive, device, level):
@@ -341,14 +386,13 @@
     def _():
         steps(lambda step: far_copy(step).start())
 
-    shadow_do(lambda copy: copy.start())
-
     def row_copies(step):
         if step != 0:
             radial_copy(step).start()
         near_copy(step).start()
 
     steps(row_copies)
+    shadow_do(lambda copy: copy.start())
 
     for index in range(5, 9):
         inputs[index].wait()
@@ -469,6 +513,22 @@
             field[which, i, PAD : PAD + cells] = jnp.where(keep, middle[i], 0.0)
 
     set_faces(0, phi, row)
+    column_copy = remote(
+        sums.at[0], sums_column.at[depth], column_send, column_recv.at[depth], early_phi, 0
+    )
+
+    def wait_rows(step):
+        if step != 0:
+            arrival(mid, radial_recv, step).wait_recv()
+        arrival(near_ghost, nghost_recv, step).wait_recv()
+
+    @pl.when(half == 1)
+    def _():
+        steps(wait_rows)
+        assemble(0, mid, near_ghost, None, row)
+        evaluate(0, row)
+        sums[0] = jnp.where(is_second, 0.0, inner_sums(0, 1))
+        column_copy.start()
 
     wide = (slots, slots)
     from_slot = lax.broadcasted_iota(jnp.int32, wide, 0)
@@ -509,61 +569,63 @@
     )
     part[...] = product.reshape(2, cells, width)
 
-    main_copy = remote(part, main.at[depth], part_send.at[0], main_recv.at[depth], early_phi, 0)
+    def child_copy(slot):
+        return remote(part, main.at[slot], part_send.at[0], main_recv.at[slot], phi, row)
+
+    for index in range(2):
+
+        @pl.when(has_child[index])
+        def _():
+            child_copy(index).wait_recv()
+            part[...] += main[index]
+
+    main_copy = remote(
+        part,
+        main.at[tree_slot],
+        part_send.at[0],
+        main_recv.at[tree_slot],
+        phi_of(here, parent_half),
+        parent_row,
+    )
     near_part_copy = remote(
         part.at[:, pl.ds(near_src, PAD)],
-        near_part.at[depth],
+        near_part.at[feeder_slot],
         part_send.at[1],
-        near_recv.at[depth],
+        near_recv.at[feeder_slot],
         early_twin_phi,
         0,
     )
     far_part_copy = remote(
         part.at[1, pl.ds(far_src, PAD)],
-        far_part.at[depth],
+        far_part.at[feeder_slot],
         part_send.at[2],
-        far_recv.at[depth],
+        far_recv.at[feeder_slot],
         far_of_late,
         0,
     )
-    far_part_copy.start()
-    near_part_copy.start()
 
     @pl.when(depth != 0)
     def _():
         main_copy.start()
 
-    def wait_rows(step):
-        if step != 0:
-            arrival(mid, radial_recv, step).wait_recv()
-        arrival(near_ghost, nghost_recv, step).wait_recv()
-
-    steps(wait_rows)
+    @pl.when(jnp.logical_or(is_feeder, is_root))
+    def _():
+        far_part_copy.start()
+        near_part_copy.start()
 
     @pl.when(half == 0)
     def _():
-        def back(step):
-            arrival(far_ghost, fghost_recv, step).wait_recv()
-            far_copy(step).start()
-
-        steps(back)
+        steps(wait_rows)
+        steps(lambda step: arrival(far_ghost, fghost_recv, step).wait_recv())
         assemble(0, mid, near_ghost, far_ghost, row)
-
-    @pl.when(half == 1)
-    def _():
-        assemble(0, mid, near_ghost, None, row)
-
-    evaluate(0, row)
-
-    column_copy = remote(
-        sums.at[0], sums_column.at[depth], column_send, column_recv.at[depth], early_phi, 0
-    )
-
-    @pl.when(depth != 0)
-    def _():
-        own = inner_sums(0, half)
-        sums[0] = jnp.where(is_second, 0.0, own)
-        column_copy.start()
+        evaluate(0, row)
+
+        @pl.when(depth != 0)
+        def _():
+            sums[0] = inner_sums(0, 0)
+            column_copy.start()
+
+        steps(lambda step: far_copy(step).start())
 
     def total_copy(z):
         return remote(
@@ -597,11 +659,10 @@
         0,
     )
 
-    def send_fields():
-        copy = pltpu.make_async_copy(
-            values.at[0, :, EDGE : EDGE + layers, PAD : PAD + cells], fields_out, out_sem.at[0]
-        )
-        return copy
+    def keep_fields():
+        for kind in range(5):
+            for layer in range(layers):
+                fields_out[kind, layer] = values[0, kind, EDGE + layer, PAD : PAD + cells]
 
     def sides(near_value, far_value):
         return (
@@ -617,7 +678,6 @@
                 copy.wait_recv()
         assemble(1, shadow_mid, shadow_near, None, 0)
         evaluate(1, 0)
-        main[0] = part[...]
 
         @pl.loop(1, column)
         def _(z):
@@ -625,22 +685,19 @@
                 sums.at[0], sums_column.at[z], column_send, column_recv.at[z], phi, 0
             ).wait_recv()
 
-        @pl.loop(0, column)
-        def _(z):
+        middle, nears, fars = part[...], None, None
+        for _z, slot in feeders:
             remote(
-                near_part.at[z], near_part.at[z], part_send.at[1], near_recv.at[z], phi, 0
+                near_part.at[slot], near_part.at[slot], part_send.at[1], near_recv.at[slot], phi, 0
             ).wait_recv()
             remote(
-                far_part.at[z], far_part.at[z], part_send.at[2], far_recv.at[z], phi, 0
+                far_part.at[slot], far_part.at[slot], part_send.at[2], far_recv.at[slot], phi, 0
             ).wait_recv()
-
-            @pl.when(z != 0)
-            def _():
-                remote(part, main.at[z], part_send.at[0], main_recv.at[z], phi, 0).wait_recv()
-
-        middle = jnp.sum(main[...], axis=0)
-        nears = jnp.sum(near_part[...], axis=0)
-        fars = jnp.sum(far_part[...], axis=0)
+            nears = near_part[slot] if nears is None else nears + near_part[slot]
+            fars = far_part[slot] if fars is None else fars + far_part[slot]
+            if slot:
+                child_copy(slot - 1).wait_recv()
+                middle = middle + main[slot - 1]
         for which in (0, 1):
             low, high = sides(nears[which], fars if which == 0 else jnp.zeros_like(fars))
             bound[which, 0:PAD] = low
@@ -658,7 +715,7 @@
 
         forward_copy.start()
         far_forward_copy.start()
-        send_fields().start()
+        keep_fields()
 
         @pl.loop(1, planes)
         def _(step):
@@ -690,7 +747,7 @@
 
     @pl.when(depth != 0)
     def _():
-        send_fields().start()
+        keep_fields()
         remote(totals, totals, total_send.at[0], total_recv, phi, 0).wait_recv()
 
     total = totals[...]
@@ -707,7 +764,6 @@
     coef_out[0:1] = jnp.broadcast_to(along, (1, width))
     coef_out[1:2] = jnp.broadcast_to(across, (1, width))
 
-    send_fields().wait()
     weight_copy.wait_send()
 
     @pl.loop(1, planes)
@@ -722,8 +778,11 @@
 
     steps(sent_rows)
     shadow_do(lambda copy: copy.wait_send())
-    near_part_copy.wait_send()
-    far_part_copy.wait_send()
+
+    @pl.when(jnp.logical_or(is_feeder, is_root))
+    def _():
+        near_part_copy.wait_send()
+        far_part_copy.wait_send()
 
     @pl.when(depth != 0)
     def _():
@@ -779,11 +838,11 @@
     fields, coef = pl.pallas_call(
         functools.partial(kernel, phis, rows),
         out_shape=(
-            jax.ShapeDtypeStruct((5,) + start_field.shape, F32),
-            jax.ShapeDtypeStruct((2, width), F32),
+            pltpu.VMEM((5,) + start_field.shape, F32),
+            pltpu.VMEM((2, width), F32),
         ),
         in_specs=[anywhere] * 9,
-        out_specs=(anywhere, pl.BlockSpec(memory_space=pltpu.VMEM)),
+        out_specs=(pl.BlockSpec(memory_space=pltpu.VMEM),) * 2,
         scratch_shapes=local
         + [
             pltpu.VMEM((planes, 2 * CAP, width), BF16),
@@ -791,9 +850,9 @@
             pltpu.VMEM((cells, planes * CAP), BF16),
             pltpu.VMEM((cells, planes * CAP), BF16),
             pltpu.VMEM((2, cells, width), F32),
-            pltpu.VMEM((column, 2, cells, width), F32),
-            pltpu.VMEM((column, 2, PAD, width), F32),
-            pltpu.VMEM((column, PAD, width), F32),
+            pltpu.VMEM((6, 2, cells, width), F32),
+            pltpu.VMEM((7, 2, PAD, width), F32),
+            pltpu.VMEM((7, PAD, width), F32),
             pltpu.VMEM((2, tall, width), F32),
             pltpu.VMEM((tall, width), F32),
             pltpu.VMEM((PAD, width), F32),
@@ -811,15 +870,14 @@
             pltpu.VMEM((planes, 1, width), F32),
             pltpu.VMEM((1, width), F32),
             dma((9,)),
-            dma((1,)),
             dma((planes,)),
             dma((planes,)),
             dma,
             dma,
             dma((3,)),
-            dma((column,)),
-            dma((column,)),
-            dma((column,)),
+            dma((6,)),
+            dma((7,)),
+            dma((7,)),
             dma((2,)),
             dma((2,)),
             dma((3,)),

time: 58.3 us -> 48.5 us (0.83)
  Pallas kernels: 55 us -> 46.9 us
  other arithmetic: 1.79 us -> 0.71 us
  local copies, waits for them, and re-layouts: 0.63 us -> 0.01 us
    pallas_call x1, Pallas kernels: 55 us -> 46.9 us  [body(): pl.pallas_call(functools.partial(kernel, phis, rows), out_shape=(pltpu.VM...]
    add x1, other arithmetic: 1.79 us -> 0.71 us  [body(): residual = fields[0] - along * fields[2] + across * fields[4]]
    unnamed x4 -> x2, local copies, waits for them, and re-layouts: 0.63 us -> 0.01 us
where the time goes in v3:
time: 48.5 us; the launch traced here: 48.3 us
  Pallas kernels  46.9 us (97%)
  other arithmetic  0.71 us (1%)
  between operations  0.66 us (1%)
    pallas_call x1, Pallas kernels, body(): pl.pallas_call(functools.partial(kernel, phis, rows), out_shape=(pltpu.VM...  46.9 us

profile of v3, /device:TPU:1, one launch (start us, length us, event | category | flops | bytes accessed | tf_op | source)
XLA Modules:
  0.0 48.3 jit_solution(4195394577808173025)
XLA Ops:
  0.6 0.0 copy-start
  0.6 46.9 %shard_map.104 = (f32[5,4,48,128]{3,2,1,0:T(8,128)S(1)}, f32[2,128]{1,0:T(2,128)S(1)}) custom-call(bf16[256,128]{1,0:T(8,128)(2,1)} %mag_hbm.1, s32[1,256]{1,0:T(1,128)} %bitcast.33, s32[1,256]{1,0:T(1,128)} %bitcast.34, bf16[48,512]{1,0:T(8,128)(2,1)} %bitcast.31, bf16[128,128]{1,0:T(8,128)(2,1)} %theta_hbm.1, f32[32]{0:T(128)} %radial_hbm.1, ...), custom_call_target="tpu_custom_call" | custom-call | tf_op jit(solution)/shard_map/pallas_call | solution.py:838
  47.6 0.0 copy-done
  47.6 0.7 %fusion = (f32[4,48,128]{2,1,0:T(8,128)}, f32[4,48,128]{2,1,0:T(8,128)}) fusion(f32[5,4,48,128]{3,2,1,0:T(8,128)S(1)} %get-tuple-element.5, f32[128]{0:T(128)S(1)} %get-tuple-element.9, f32[128]{0:T(128)S(1)} %get-tuple-element.8, f32[4,48,128]{2,1,0:T(8,128)S(1)} %copy-done), kind=kLoop, calls=%fused_computation.1 | loop fusion | flops 196608 | bytes 787456 | tf_op jit(solution)/shard_map/add | solution.py:902
  (1 shorter events, 0.0 us)
Async XLA Ops:
  0.6 47.0 %copy-start = (f32[4,48,128]{2,1,0:T(8,128)S(1)}, f32[4,48,128]{2,1,0:T(8,128)}, u32[]{:S(2)}) copy-start(f32[4,48,128]{2,1,0:T(8,128)} %start_hbm.1) | copy-start | bytes 294916

commit v4 on v3

--- a/solution.py
+++ b/solution.py
@@ -55,8 +55,8 @@
     mid,
     near_ghost,
     far_ghost,
-    shadow_mid,
-    shadow_near,
+    lend,
+    lent,
     field,
     inverse,
     faces,
@@ -82,8 +82,8 @@
     nghost_recv,
     fghost_send,
     fghost_recv,
-    shadow_send,
-    shadow_recv,
+    lend_send,
+    lend_recv,
     column_send,
     column_recv,
     plane_send,
@@ -109,41 +109,40 @@
     is_root = depth == 0
     is_second = depth == rows
 
-    offsets = (1, 2, 4)
-    reach = jnp.where(half == 0, row, column - depth)
-    bit = jnp.where(
-        lax.rem(reach, 2) == 1, 1, jnp.where(lax.rem(reach, 4) == 2, 2, 4)
-    ).astype(jnp.int32)
-    bit = jnp.where(reach == rows, 2, bit).astype(jnp.int32)
-    parent_reach = jnp.where(reach == rows, rows - 2, reach - bit).astype(jnp.int32)
-    is_feeder = jnp.logical_and(parent_reach == 0, depth != 0)
-    parent_half = jnp.where(parent_reach == 0, 0, half).astype(jnp.int32)
-    parent_depth = jnp.where(half == 0, parent_reach, column - parent_reach)
-    parent_depth = jnp.where(parent_reach == 0, 0, parent_depth).astype(jnp.int32)
+    above = {1: 0, 2: 0, 3: 2, 4: 2, 5: 6, 6: 0, 7: 6, 8: 6}
+    parents = {z: above[z] for z in range(1, rows)}
+    parents.update({column - d: (column - above[d]) % column for d in range(1, rows + 1)})
+    children = {z: [c for c in sorted(parents) if parents[c] == z] for z in range(column)}
+
+    def table(entries):
+        result = 0
+        for z, entry in entries.items():
+            if entry:
+                result = jnp.where(depth == z, entry, result).astype(jnp.int32)
+        return result
+
+    parent_depth = table(parents)
+    parent_half = jnp.where(parent_depth >= rows, 1, 0).astype(jnp.int32)
     parent_row = parent_depth - parent_half * rows
-    tree_slot = lax.div(bit, 2) + jnp.where(is_feeder, 3 * half, 0).astype(jnp.int32)
-    inner = jnp.logical_and(reach > 0, reach < rows)
-    has_child = (
-        jnp.logical_and(inner, jnp.logical_and(lax.rem(reach, 2) == 0, reach + 1 < rows)),
-        jnp.logical_and(
-            inner,
-            jnp.logical_or(
-                jnp.logical_and(lax.rem(reach, 4) == 0, reach + 2 < rows),
-                jnp.logical_and(half == 1, reach == rows - 2),
-            ),
-        ),
-    )
-    child_depth = [
-        jnp.where(half == 0, depth + offset, depth - offset).astype(jnp.int32)
-        for offset in offsets[:2]
+    tree_slot = table({z: children[p].index(z) for z, p in parents.items()})
+    is_feeder = jnp.logical_and(parent_depth == 0, depth != 0)
+    feeders = [(0, 0)] + [(z, 1 + slot) for slot, z in enumerate(children[0])]
+    feeder_slot = jnp.where(is_feeder, 1 + tree_slot, 0).astype(jnp.int32)
+    most = max(len(children[z]) for z in range(1, column))
+    has_child = [
+        table({z: len(children[z]) > index for z in range(1, column)}) > 0
+        for index in range(most)
     ]
-    feeders = [(0, 0)]
-    for index, offset in enumerate(offsets):
-        if offset < rows:
-            feeders += [(offset, 1 + index), (column - offset, 4 + index)]
-        elif offset == rows == 2:
-            feeders.append((column - offset, 4 + index))
-    feeder_slot = jnp.where(is_feeder, 1 + tree_slot, 0).astype(jnp.int32)
+    child_row = [
+        table(
+            {
+                z: children[z][index] % rows
+                for z in range(1, column)
+                if len(children[z]) > index
+            }
+        )
+        for index in range(most)
+    ]
 
     def phi_of(place, side):
         return lax.div(place, 2) * 4 + side * 2 + lax.rem(place, 2)
@@ -164,6 +163,29 @@
     last = cells - PAD
     near_src = pl.multiple_of((1 - core) * last, PAD)
     far_src = pl.multiple_of(core * last, PAD)
+
+    has_next = row < rows - 1
+    has_previous = row > 0
+
+    def steps(act):
+        act(0)
+
+        @pl.when(has_next)
+        def _():
+            act(1)
+
+        @pl.when(has_previous)
+        def _():
+            act(-1)
+
+    barrier = pltpu.get_barrier_semaphore()
+
+    def greet(device, level):
+        pl.semaphore_signal(barrier, inc=1, device_id=(device, level), device_id_type=MESH)
+
+    @pl.loop(1, planes)
+    def _(step):
+        greet(phi_of(lax.rem(here + step, planes), half), row)
 
     inputs = [
         pltpu.make_async_copy(src, dst, in_sem.at[index])
@@ -184,29 +206,6 @@
     for copy in inputs:
         copy.start()
 
-    has_next = row < rows - 1
-    has_previous = row > 0
-
-    def steps(act):
-        act(0)
-
-        @pl.when(has_next)
-        def _():
-            act(1)
-
-        @pl.when(has_previous)
-        def _():
-            act(-1)
-
-    barrier = pltpu.get_barrier_semaphore()
-
-    def greet(device, level):
-        pl.semaphore_signal(barrier, inc=1, device_id=(device, level), device_id_type=MESH)
-
-    @pl.loop(1, planes)
-    def _(step):
-        greet(phi_of(lax.rem(here + step, planes), half), row)
-
     greet(phi_of(here, other), lax.rem(row + rows - rows // 2, rows))
 
     def greet_rows(step):
@@ -218,7 +217,7 @@
 
     @pl.when(half == 0)
     def _():
-        steps(lambda step: greet(far, row + step))
+        greet(far, row)
 
     @pl.when(is_root)
     def _():
@@ -227,18 +226,15 @@
             greet(phi_of(twin, side), level)
             greet(phi_of(place_of(far_of_early), side), level)
 
-        for step in (0, 1):
-            greet(phi_of(twin, 1), step)
-
         @pl.loop(1, column)
         def _(z):
             greet(phi_of(here, lax.div(z, rows)), lax.rem(z, rows))
 
-    for index in range(2):
+    for index in range(most):
 
         @pl.when(has_child[index])
         def _():
-            greet(phi, child_depth[index] - half * rows)
+            greet(phi, child_row[index])
 
     for index in range(3):
         inputs[index].wait()
@@ -268,11 +264,10 @@
         (planes - 1)
         + 1
         + 2 * (flag(has_next) + flag(has_previous))
-        + half * (1 + flag(has_next) + flag(has_previous))
+        + half
         + flag(depth != 0)
         + 2 * flag(jnp.logical_or(is_feeder, is_root))
-        + flag(jnp.logical_and(depth != 0, parent_reach != 0))
-        + flag(jnp.logical_or(depth == rows, depth == rows + 1)),
+        + flag(parent_depth != 0),
     )
 
     def remote(src, dst, send, receive, device, level):
@@ -289,20 +284,6 @@
         wsend, wrecv, w_send, w_recv, phi_of(here, other), lax.rem(row + rows // 2, rows)
     )
     weight_copy.start()
-
-    def pack_copy(place, slot):
-        return remote(
-            pack.at[place],
-            recv.at[slot],
-            pack_send.at[place],
-            pack_recv.at[slot],
-            phi_of(place, half),
-            row,
-        )
-
-    @pl.loop(1, planes)
-    def _(step):
-        pack_copy(lax.rem(here + step, planes), here).start()
 
     def layers_of(step):
         if step == 0:
@@ -335,14 +316,33 @@
 
     def far_copy(step):
         source, ghost = layers_of(step)
+        if step == 0:
+            return remote(
+                mid.at[source, pl.ds(far_src, PAD)],
+                far_ghost.at[ghost],
+                fghost_send.at[1],
+                fghost_recv.at[1],
+                far,
+                row,
+            )
         return remote(
-            mid.at[source, pl.ds(far_src, PAD)],
+            far_ghost.at[source],
             far_ghost.at[ghost],
             fghost_send.at[1 + step],
             fghost_recv.at[1 - step],
-            far,
+            phi,
             row + step,
         )
+
+    def pass_far(step):
+        if step == 0:
+            arrival(far_ghost, fghost_recv, 0).wait_recv()
+        else:
+            far_copy(step).start()
+
+    def wait_passed(step):
+        if step != 0:
+            arrival(far_ghost, fghost_recv, step).wait_recv()
 
     def arrival(buffer, semaphore, step):
         _, ghost = layers_of(-step)
@@ -350,41 +350,32 @@
             buffer.at[ghost], buffer.at[ghost], w_send, semaphore.at[1 + step], near, row
         )
 
-    def shadow_copies(step):
-        if step == 0:
-            source, ghost = pl.ds(EDGE, layers), pl.ds(EDGE, layers)
-        else:
-            source, ghost = pl.ds(EDGE, EDGE), pl.ds(EDGE + layers, EDGE)
-        return (
-            remote(
-                mid.at[source],
-                shadow_mid.at[ghost],
-                shadow_send.at[0],
-                shadow_recv.at[2 * step],
-                early_phi,
-                0,
-            ),
-            remote(
-                mid.at[source, pl.ds(near_src, PAD)],
-                shadow_near.at[ghost],
-                shadow_send.at[1],
-                shadow_recv.at[2 * step + 1],
-                early_twin_phi,
-                0,
-            ),
-        )
-
-    def shadow_do(act):
-        for step in (0, 1):
-
-            @pl.when(depth == rows + step)
-            def _():
-                for copy in shadow_copies(step):
-                    act(copy)
+    lend_copy = remote(
+        lend,
+        lent.at[:, pl.ds(PAD, cells)],
+        lend_send,
+        lend_recv,
+        early_phi,
+        0,
+    )
 
     @pl.when(half == 1)
     def _():
-        steps(lambda step: far_copy(step).start())
+        far_copy(0).start()
+
+    def pack_copy(place, slot):
+        return remote(
+            pack.at[place],
+            recv.at[slot],
+            pack_send.at[place],
+            pack_recv.at[slot],
+            phi_of(place, half),
+            row,
+        )
+
+    @pl.loop(1, planes)
+    def _(step):
+        pack_copy(lax.rem(here + step, planes), here).start()
 
     def row_copies(step):
         if step != 0:
@@ -392,7 +383,6 @@
         near_copy(step).start()
 
     steps(row_copies)
-    shadow_do(lambda copy: copy.start())
 
     for index in range(5, 9):
         inputs[index].wait()
@@ -484,22 +474,55 @@
     cell_index = lax.broadcasted_iota(jnp.int32, (tall, width), 0)
     lane = lax.broadcasted_iota(jnp.int32, (1, width), 1)
 
-    def inner_sums(which, side):
+    def four_sums(terms, side):
         reach = EDGE * (1 - 2 * side)
         low = PAD - (1 - core) * reach
         high = PAD + cells + core * reach
         counted = jnp.logical_and(cell_index >= low, cell_index < high)
         result = jnp.zeros((1, width), F32)
-        for index, (left, right) in enumerate(((0, 1), (1, 2), (2, 3), (3, 4))):
-            total = None
-            for i in range(EDGE, EDGE + layers):
-                product = values[which, left, i] * values[which, right, i]
-                total = product if total is None else total + product
+        for index, total in enumerate(terms):
             total = jnp.where(counted, total, 0.0)
             total = jnp.sum(total, axis=0, keepdims=True)
             total = jnp.sum(total, axis=1, keepdims=True)
             result = jnp.where(lane == index, total, result)
         return result
+
+    def inner_sums(which, side):
+        terms = []
+        for left, right in ((0, 1), (1, 2), (2, 3), (3, 4)):
+            total = None
+            for i in range(EDGE, EDGE + layers):
+                product = values[which, left, i] * values[which, right, i]
+                total = product if total is None else total + product
+            terms.append(total)
+        return four_sums(terms, side)
+
+    def boundary_sums(which, boundary, fields, side):
+        radial = radial_faces(0)
+        zero = jnp.zeros_like(boundary)
+        added = radial[EDGE] * boundary
+        scaled = added * inverse[which, EDGE]
+
+        def first(i):
+            return scaled if i == EDGE else zero
+
+        image0, image1 = (image(which, radial, first, EDGE + i) for i in (0, 1))
+        image_scaled = (image0 * inverse[which, EDGE], image1 * inverse[which, EDGE + 1])
+
+        def second(i):
+            return image_scaled[i - EDGE] if i in (EDGE, EDGE + 1) else zero
+
+        last0, last1 = (image(which, radial, second, EDGE + i) for i in (0, 1))
+        return four_sums(
+            (
+                added * (2.0 * fields[0] + scaled),
+                2.0 * added * fields[1] + scaled * image0,
+                2.0 * scaled * fields[2] + image0 * image_scaled[0] + image1 * image_scaled[1],
+                image_scaled[0] * (2.0 * fields[2] + last0)
+                + image_scaled[1] * (2.0 * fields[3] + last1),
+            ),
+            side,
+        )
 
     def assemble(which, middle, near_cells, far_cells, level):
         for i in range(deep):
@@ -522,12 +545,11 @@
             arrival(mid, radial_recv, step).wait_recv()
         arrival(near_ghost, nghost_recv, step).wait_recv()
 
-    @pl.when(half == 1)
-    def _():
+    def late_sums():
         steps(wait_rows)
         assemble(0, mid, near_ghost, None, row)
         evaluate(0, row)
-        sums[0] = jnp.where(is_second, 0.0, inner_sums(0, 1))
+        sums[0] = inner_sums(0, 1)
         column_copy.start()
 
     wide = (slots, slots)
@@ -572,13 +594,6 @@
     def child_copy(slot):
         return remote(part, main.at[slot], part_send.at[0], main_recv.at[slot], phi, row)
 
-    for index in range(2):
-
-        @pl.when(has_child[index])
-        def _():
-            child_copy(index).wait_recv()
-            part[...] += main[index]
-
     main_copy = remote(
         part,
         main.at[tree_slot],
@@ -604,28 +619,60 @@
         0,
     )
 
-    @pl.when(depth != 0)
-    def _():
-        main_copy.start()
-
-    @pl.when(jnp.logical_or(is_feeder, is_root))
-    def _():
-        far_part_copy.start()
-        near_part_copy.start()
+    def send_part():
+        @pl.when(depth != 0)
+        def _():
+            main_copy.start()
+
+        @pl.when(jnp.logical_or(is_feeder, is_root))
+        def _():
+            far_part_copy.start()
+            near_part_copy.start()
+
+    is_leaf = jnp.logical_not(has_child[0]) if most else row >= 0
+
+    @pl.when(is_leaf)
+    def _():
+        send_part()
 
     @pl.when(half == 0)
     def _():
+        steps(pass_far)
+
+    for index in range(most):
+
+        @pl.when(has_child[index])
+        def _():
+            child_copy(index).wait_recv()
+            part[...] += main[index]
+
+    @pl.when(jnp.logical_not(is_leaf))
+    def _():
+        send_part()
+
+    @pl.when(half == 1)
+    def _():
+        late_sums()
+
+        @pl.when(is_second)
+        def _():
+            for index, (kind, i) in enumerate(((1, EDGE), (3, EDGE), (4, EDGE), (4, EDGE + 1))):
+                lend[index] = values[0, kind, i, PAD : PAD + cells]
+            lend_copy.start()
+
+    @pl.when(half == 0)
+    def _():
         steps(wait_rows)
-        steps(lambda step: arrival(far_ghost, fghost_recv, step).wait_recv())
+        steps(wait_passed)
         assemble(0, mid, near_ghost, far_ghost, row)
         evaluate(0, row)
 
+        sums[0] = inner_sums(0, 0)
+
         @pl.when(depth != 0)
         def _():
-            sums[0] = inner_sums(0, 0)
             column_copy.start()
-
-        steps(lambda step: far_copy(step).start())
+            far_copy(0).start()
 
     def total_copy(z):
         return remote(
@@ -673,11 +720,7 @@
     @pl.when(is_root)
     def _():
         set_faces(1, late_phi, 0)
-        for step in (0, 1):
-            for copy in shadow_copies(step):
-                copy.wait_recv()
-        assemble(1, shadow_mid, shadow_near, None, 0)
-        evaluate(1, 0)
+        lend_copy.wait_recv()
 
         @pl.loop(1, column)
         def _(z):
@@ -703,8 +746,12 @@
             bound[which, 0:PAD] = low
             bound[which, PAD : PAD + cells] = middle[which]
             bound[which, PAD + cells : tall] = high
-            add_boundary(which, bound[which])
-        sums_column[0] = inner_sums(0, 0) + inner_sums(1, 1)
+        own_fields = (values[0, 1, EDGE], values[0, 3, EDGE], values[0, 4, EDGE], values[0, 4, EDGE + 1])
+        sums_column[0] = (
+            sums[0]
+            + boundary_sums(0, bound[0], own_fields, 0)
+            + boundary_sums(1, bound[1], [lent[index] for index in range(4)], 1)
+        )
         mine = jnp.sum(sums_column[...], axis=0)
         sums[1] = mine
         sums_plane[here] = mine
@@ -713,8 +760,10 @@
         def _(step):
             plane_copy(lax.rem(here + step, planes), here).start()
 
+        far_copy(0).start()
         forward_copy.start()
         far_forward_copy.start()
+        add_boundary(0, bound[0])
         keep_fields()
 
         @pl.loop(1, planes)
@@ -730,7 +779,8 @@
 
     @pl.when(half == 1)
     def _():
-        steps(lambda step: arrival(far_ghost, fghost_recv, step).wait_recv())
+        steps(pass_far)
+        steps(wait_passed)
         assemble(0, mid, near_ghost, far_ghost, row)
         evaluate(0, row)
 
@@ -777,7 +827,11 @@
         far_copy(step).wait_send()
 
     steps(sent_rows)
-    shadow_do(lambda copy: copy.wait_send())
+
+    @pl.when(is_second)
+    def _():
+        lend_copy.wait_send()
+
 
     @pl.when(jnp.logical_or(is_feeder, is_root))
     def _():
@@ -859,12 +913,12 @@
             pltpu.VMEM((deep, cells, width), F32),
             pltpu.VMEM((deep, PAD, width), F32),
             pltpu.VMEM((deep, PAD, width), F32),
-            pltpu.VMEM((deep, cells, width), F32),
-            pltpu.VMEM((deep, PAD, width), F32),
-            pltpu.VMEM((2, deep, tall, width), F32),
+            pltpu.VMEM((4, cells, width), F32),
+            pltpu.VMEM((4, tall, width), F32),
+            pltpu.VMEM((1, deep, tall, width), F32),
             pltpu.VMEM((2, deep, tall, width), F32),
             pltpu.VMEM((2, 2, tall, width), F32),
-            pltpu.VMEM((2, 5, deep, tall, width), F32),
+            pltpu.VMEM((1, 5, deep, tall, width), F32),
             pltpu.VMEM((2, 1, width), F32),
             pltpu.VMEM((column, 1, width), F32),
             pltpu.VMEM((planes, 1, width), F32),
@@ -886,8 +940,8 @@
             dma((3,)),
             dma((3,)),
             dma((3,)),
-            dma((2,)),
-            dma((4,)),
+            dma,
+            dma,
             dma,
             dma((column,)),
             dma((planes,)),

time: 48.5 us -> 44.9 us (0.926)
  Pallas kernels: 46.9 us -> 43.3 us
    pallas_call x1, Pallas kernels: 46.9 us -> 43.3 us  [body(): pl.pallas_call(functools.partial(kernel, phis, rows), out_shape=(pltpu.VM...]
where the time goes in v4:
time: 44.9 us; the launch traced here: 44.7 us
  Pallas kernels  43.3 us (96%)
  other arithmetic  0.71 us (2%)
  between operations  0.66 us (1%)
    pallas_call x1, Pallas kernels, body(): pl.pallas_call(functools.partial(kernel, phis, rows), out_shape=(pltpu.VM...  43.3 us

profile of v4, /device:TPU:1, one launch (start us, length us, event | category | flops | bytes accessed | tf_op | source)
XLA Modules:
  0.0 44.7 jit_solution(1356897142325202706)
XLA Ops:
  0.6 0.0 copy-start
  0.6 43.3 %shard_map.104 = (f32[5,4,48,128]{3,2,1,0:T(8,128)S(1)}, f32[2,128]{1,0:T(2,128)S(1)}) custom-call(bf16[256,128]{1,0:T(8,128)(2,1)} %mag_hbm.1, s32[1,256]{1,0:T(1,128)} %bitcast.33, s32[1,256]{1,0:T(1,128)} %bitcast.34, bf16[48,512]{1,0:T(8,128)(2,1)} %bitcast.31, bf16[128,128]{1,0:T(8,128)(2,1)} %theta_hbm.1, f32[32]{0:T(128)} %radial_hbm.1, ...), custom_call_target="tpu_custom_call" | custom-call | tf_op jit(solution)/shard_map/pallas_call | solution.py:892
  44.0 0.0 copy-done
  44.0 0.7 %fusion = (f32[4,48,128]{2,1,0:T(8,128)}, f32[4,48,128]{2,1,0:T(8,128)}) fusion(f32[5,4,48,128]{3,2,1,0:T(8,128)S(1)} %get-tuple-element.5, f32[128]{0:T(128)S(1)} %get-tuple-element.9, f32[128]{0:T(128)S(1)} %get-tuple-element.8, f32[4,48,128]{2,1,0:T(8,128)S(1)} %copy-done), kind=kLoop, calls=%fused_computation.1 | loop fusion | flops 196608 | bytes 787456 | tf_op jit(solution)/shard_map/add | solution.py:956
  (1 shorter events, 0.0 us)
Async XLA Ops:
  0.6 43.3 %copy-start = (f32[4,48,128]{2,1,0:T(8,128)S(1)}, f32[4,48,128]{2,1,0:T(8,128)}, u32[]{:S(2)}) copy-start(f32[4,48,128]{2,1,0:T(8,128)} %start_hbm.1) | copy-start | bytes 294916

commit v5 on v4

--- a/solution.py
+++ b/solution.py
@@ -283,7 +283,6 @@
     weight_copy = remote(
         wsend, wrecv, w_send, w_recv, phi_of(here, other), lax.rem(row + rows // 2, rows)
     )
-    weight_copy.start()
 
     def layers_of(step):
         if step == 0:
@@ -362,6 +361,8 @@
     @pl.when(half == 1)
     def _():
         far_copy(0).start()
+
+    weight_copy.start()
 
     def pack_copy(place, slot):
         return remote(

time: 44.9 us -> 44.9 us (level)
  no operation moved by 1% of the time
where the time goes in v5:
time: 44.9 us; the launch traced here: 44.7 us
  Pallas kernels  43.3 us (96%)
  other arithmetic  0.71 us (2%)
  between operations  0.66 us (1%)
    pallas_call x1, Pallas kernels, body(): pl.pallas_call(functools.partial(kernel, phis, rows), out_shape=(pltpu.VM...  43.3 us

profile of v5, /device:TPU:1, one launch (start us, length us, event | category | flops | bytes accessed | tf_op | source)
XLA Modules:
  0.0 44.7 jit_solution(8101750243129002407)
XLA Ops:
  0.6 0.0 copy-start
  0.6 43.3 %shard_map.104 = (f32[5,4,48,128]{3,2,1,0:T(8,128)S(1)}, f32[2,128]{1,0:T(2,128)S(1)}) custom-call(bf16[256,128]{1,0:T(8,128)(2,1)} %mag_hbm.1, s32[1,256]{1,0:T(1,128)} %bitcast.33, s32[1,256]{1,0:T(1,128)} %bitcast.34, bf16[48,512]{1,0:T(8,128)(2,1)} %bitcast.31, bf16[128,128]{1,0:T(8,128)(2,1)} %theta_hbm.1, f32[32]{0:T(128)} %radial_hbm.1, ...), custom_call_target="tpu_custom_call" | custom-call | tf_op jit(solution)/shard_map/pallas_call | solution.py:893
  44.0 0.0 copy-done
  44.0 0.7 %fusion = (f32[4,48,128]{2,1,0:T(8,128)}, f32[4,48,128]{2,1,0:T(8,128)}) fusion(f32[5,4,48,128]{3,2,1,0:T(8,128)S(1)} %get-tuple-element.5, f32[128]{0:T(128)S(1)} %get-tuple-element.9, f32[128]{0:T(128)S(1)} %get-tuple-element.8, f32[4,48,128]{2,1,0:T(8,128)S(1)} %copy-done), kind=kLoop, calls=%fused_computation.1 | loop fusion | flops 196608 | bytes 787456 | tf_op jit(solution)/shard_map/add | solution.py:957
  (1 shorter events, 0.0 us)
Async XLA Ops:
  0.6 43.3 %copy-start = (f32[4,48,128]{2,1,0:T(8,128)S(1)}, f32[4,48,128]{2,1,0:T(8,128)}, u32[]{:S(2)}) copy-start(f32[4,48,128]{2,1,0:T(8,128)} %start_hbm.1) | copy-start | bytes 294916
